TPU v7x, 256 devices: a whole 4x4x8 slice. The times are simulated.
256 devices in a mesh: src: 32 (over y_hi, z, core), tgt: 8 (over x, y_lo).
Axes of the slice: x: 4, y: 4 (y_hi: 2, y_lo: 2; y = y_hi * 2 + y_lo), z: 8, core: 2. Of those that a mesh axis runs over, the one named last changes fastest.
Arguments:
- edge_states: bfloat16 [32, 8, 512, 1024], P('src', 'tgt'), may hold values from -6 to 6
- triplet_coeff: bfloat16 [32, 8, 16, 128, 128], P('src', 'tgt'), may hold values from -0.3984375 to 0.3984375
- block_target: int32 [32, 8, 16], P('src', 'tgt'), may hold values from 0 to 3
- block_source: int32 [32, 8, 16], P('src', 'tgt'), may hold values from 0 to 127
- block_count: int32 [32, 8], P('src', 'tgt'), may hold values from 2 to 16, as said below
- reverse_slot: int32 [32, 8, 512], P('src', 'tgt'), may hold values from 0 to 511, as said below
- w_proj: bfloat16 [2, 1024, 64], replicated, may hold values from -0.1875 to 0.1875
- w_up: bfloat16 [2, 64, 1024], replicated, may hold values from -0.75 to 0.75
- w_in: bfloat16 [2, 1024, 1024], replicated, may hold values from -0.1875 to 0.1875
- w_out: bfloat16 [2, 1024, 1024], replicated, may hold values from -0.1875 to 0.1875
- norm_gain: float32 [2, 1024], replicated, may hold values from 0.5 to 2
Outputs:
- edge_final: bfloat16 [32, 8, 512, 1024], P('src', 'tgt')
Inputs may be any that keep to these rules, and one draw needn't show every extreme that they name: `block_count`: each tile uses between 2 and 16 blocks; some tile uses all 16 in every draw. Reverse edges pair up: with C = 4, for tile (p, q) with p = a * C + r and its mirror tile (q * C + r, a), the two reverse_slot rows are inverse permutations of 0 to 511; on a tile with a = q the row is a permutation that is its own inverse without fixed points.
All inputs are finite; a program needn't handle non-finite values.
Results may differ from a plain program's by a relative error of at most 0.014.
Values may be sent and summed in bfloat16 or wider, within the bound.
A program may use at most 64 MiB of HBM per device.

v0:
```python
import jax
import jax.numpy as jnp
from jax import lax
from jax.sharding import PartitionSpec as P

BLK = 128
LAYERS = 2


def partner(value, axis, bit):
    return lax.ppermute(value, axis, [(i, i ^ 1 << bit) for i in range(lax.axis_size(axis))])


def from_everyone(value, axis):
    copies = jnp.broadcast_to(value, (lax.axis_size(axis), *value.shape))
    return lax.all_to_all(copies, axis, split_axis=0, concat_axis=0, tiled=True)


def joined_along(blocks, dim):
    blocks = jnp.moveaxis(blocks, 0, dim)
    dims = blocks.shape
    return blocks.reshape(*dims[:dim], dims[dim] * dims[dim + 1], *dims[dim + 2 :])


def gather_directly(value, axis, dim):
    blocks = from_everyone(value, axis)
    return joined_along(blocks, dim)


def bit_pairings():
    groups = lax.axis_size("tgt")
    width = groups.bit_length() - 1
    src_bits = lax.axis_size("src").bit_length() - 1
    position = lax.axis_index("src") * groups + lax.axis_index("tgt")
    pairings = []
    for bit_index in range(width):
        upper = bit_index + src_bits
        differ = position // 2**bit_index % 2 != position // 2**upper % 2
        pairings.append(((bit_index, upper), differ))
    return pairings


def mirror_inputs(values, pairings):
    carried = values
    for bit_pair, differ in pairings:
        hopped = carried
        for bit_index in bit_pair:
            hopped = partner(hopped, ("src", "tgt"), bit_index)
        carried = jnp.where(differ, hopped, carried)
    return carried


def mirror_mixed(values, pairings):
    carried = values
    for bit_pair, differ in pairings:
        hopped = carried
        for bit_index in bit_pair:
            hopped = partner(hopped, ("src", "tgt"), bit_index)
        carried = jnp.where(differ, hopped, carried)
    return carried


def triplet_sums(pooled, coeffs, targets, sources, live_count, edge_count):
    width = pooled.shape[0]
    slots = coeffs.shape[0]
    out_blocks = edge_count // BLK
    blocks = pooled.reshape(width, pooled.shape[1] // BLK, BLK)
    picked = jnp.take(blocks, sources, axis=1)
    products = jnp.einsum("cbj,bji->cbi", picked, coeffs, preferred_element_type=jnp.float32)
    live_mask = (jnp.arange(slots) < live_count).astype(jnp.float32)
    placing = (targets[:, None] == jnp.arange(out_blocks)[None, :]).astype(jnp.float32) * live_mask[
        :, None
    ]
    return jnp.einsum("cbi,bo->coi", products, placing).reshape(width, edge_count)


def transform(rows, agg_low, w_up_l, w_in_l, w_out_l, gain_l):
    summed = rows.astype(jnp.float32) + jnp.einsum(
        "ce,cd->ed", agg_low, w_up_l, preferred_element_type=jnp.float32
    )
    scale_inv = lax.rsqrt(jnp.mean(summed * summed, axis=-1, keepdims=True) + 1e-06)
    normed = (gain_l * summed * scale_inv).astype(jnp.bfloat16)
    activated = jax.nn.silu(jnp.dot(normed, w_in_l, preferred_element_type=jnp.float32)).astype(
        jnp.bfloat16
    )
    branch = jnp.dot(activated, w_out_l, preferred_element_type=jnp.float32).astype(jnp.bfloat16)
    return (summed, branch)


def local(
    edge_states,
    triplet_coeff,
    block_target,
    block_source,
    block_count,
    reverse_slot,
    w_proj,
    w_up,
    w_in,
    w_out,
    norm_gain,
):
    state = edge_states[0, 0]
    coeffs = triplet_coeff[0, 0]
    targets = block_target[0, 0]
    sources = block_source[0, 0]
    live_count = block_count[0, 0]
    reverse_rows = reverse_slot[0, 0]
    edge_count = state.shape[0]
    pairings = bit_pairings()
    mirrored = jnp.take(mirror_inputs(state, pairings), reverse_rows, axis=0)
    for layer_index in range(LAYERS):
        projected = jnp.einsum(
            "ed,dc->ce", state, w_proj[layer_index], preferred_element_type=jnp.float32
        ).astype(jnp.bfloat16)
        pooled = gather_directly(projected, "src", 1)
        agg_low = triplet_sums(pooled, coeffs, targets, sources, live_count, edge_count).astype(
            jnp.bfloat16
        )
        summed, branch = transform(
            state,
            agg_low,
            w_up[layer_index],
            w_in[layer_index],
            w_out[layer_index],
            norm_gain[layer_index],
        )
        agg_mirror = jnp.take(mirror_mixed(agg_low, pairings), reverse_rows, axis=1)
        summed_mirror, branch_mirror = transform(
            mirrored,
            agg_mirror,
            w_up[layer_index],
            w_in[layer_index],
            w_out[layer_index],
            norm_gain[layer_index],
        )
        state = (summed + branch.astype(jnp.float32) + branch_mirror.astype(jnp.float32)).astype(
            jnp.bfloat16
        )
        mirrored = (
            summed_mirror + branch_mirror.astype(jnp.float32) + branch.astype(jnp.float32)
        ).astype(jnp.bfloat16)
    return state[None, None]


def solution(mesh):
    return jax.shard_map(
        local,
        mesh=mesh,
        in_specs=(
            P("src", "tgt", None, None),
            P("src", "tgt", None, None, None),
            P("src", "tgt", None),
            P("src", "tgt", None),
            P("src", "tgt"),
            P("src", "tgt", None),
            P(),
            P(),
            P(),
            P(),
            P(),
        ),
        out_specs=P("src", "tgt", None, None),
        check_vma=False,
    )
```

profile of v0, /device:TPU:1, one launch (start us, length us, event | category | flops | bytes accessed | tf_op | source)
XLA Modules:
  0.0 390.6 jit_solution(9242824833392571879)
XLA Ops:
  3.3 12.9 %all-to-all-start = ((bf16[32,64,512]{2,1,0:T(8,128)(2,1)}), bf16[32,64,512]{2,1,0:T(8,128)(2,1)}, u32[]{:S(2)}, u32[]{:S(2)}) async-start(bf16[32,64,512]{2,1,0:T(8,128)(2,1)} %broadcast_in_dim.45), calls=%async_computation | async-start | bytes 4194304 | tf_op jit(solution)/shard_map/all_to_all | solution.py:16
  16.8 43.9 %collective-permute-done = bf16[512,1024]{1,0:T(8,128)(2,1)S(1)} collective-permute-done((bf16[512,1024]{1,0:T(8,128)(2,1)S(1)}, bf16[512,1024]{1,0:T(8,128)(2,1)S(1)}, u32[]{:S(2)}, u32[]{:S(2)}) %collective-permute-start) | collective-permute-done | bytes 1048608 | tf_op jit(solution)/shard_map/ppermute | solution.py:11
  60.7 4.0 %collective-permute-start.1 = (bf16[512,1024]{1,0:T(8,128)(2,1)S(1)}, bf16[512,1024]{1,0:T(8,128)(2,1)}, u32[]{:S(2)}, u32[]{:S(2)}) collective-permute-start(bf16[512,1024]{1,0:T(8,128)(2,1)S(1)} %collective-permute-done), channel_id=1, source_target_pairs={{0,32},{1,33},{2,34},{3,35},{4,36},{5,37},{6,38},{7,39},{8,40},{9,... | collective-permute-start | bytes 3145736 | tf_op jit(solution)/shard_map/ppermute | solution.py:11
  65.4 45.8 %collective-permute-done.1 = bf16[512,1024]{1,0:T(8,128)(2,1)} collective-permute-done((bf16[512,1024]{1,0:T(8,128)(2,1)S(1)}, bf16[512,1024]{1,0:T(8,128)(2,1)}, u32[]{:S(2)}, u32[]{:S(2)}) %collective-permute-start.1) | collective-permute-done | bytes 1048608 | tf_op jit(solution)/shard_map/ppermute | solution.py:11
  112.6 22.9 %collective-permute-done.2 = bf16[512,1024]{1,0:T(8,128)(2,1)} collective-permute-done((bf16[512,1024]{1,0:T(8,128)(2,1)S(1)}, bf16[512,1024]{1,0:T(8,128)(2,1)}, u32[]{:S(2)}, u32[]{:S(2)}) %collective-permute-start.2) | collective-permute-done | bytes 1048608 | tf_op jit(solution)/shard_map/ppermute | solution.py:11
  135.6 5.3 %collective-permute-start.3 = (bf16[512,1024]{1,0:T(8,128)(2,1)}, bf16[512,1024]{1,0:T(8,128)(2,1)}, u32[]{:S(2)}, u32[]{:S(2)}) collective-permute-start(bf16[512,1024]{1,0:T(8,128)(2,1)} %collective-permute-done.2), channel_id=1, source_target_pairs={{0,64},{1,65},{2,66},{3,67},{4,68},{5,69},{6,70},{7,71},{8,72},{9,... | collective-permute-start | bytes 3145736 | tf_op jit(solution)/shard_map/ppermute | solution.py:11
  140.9 4.1 %copy.22 = bf16[64,32,512]{2,1,0:T(8,128)(2,1)} copy(bf16[64,32,512]{2,0,1:T(8,128)(2,1)} %bitcast.6) | data formatting | bytes 4194304 | tf_op jit(solution)/shard_map/transpose | solution.py:20
  144.9 4.4 %reshape_reshape.6 = bf16[64,128,128]{2,1,0:T(8,128)(2,1)} reshape(bf16[64,32,512]{2,1,0:T(8,128)(2,1)} %copy.22) | data formatting | bytes 4194304 | tf_op jit(solution)/shard_map/reshape;reshape | solution.py:67
  149.3 4.3 %copy.23 = bf16[64,128,128]{2,0,1:T(8,128)(2,1)} copy(bf16[64,128,128]{2,1,0:T(8,128)(2,1)} %reshape_reshape.6) | data formatting | bytes 4194304 | tf_op jit(solution)/shard_map/reshape;reshape | solution.py:67
  158.9 2.8 collective-permute-done.6
  161.6 13.9 %collective-permute-done.3 = bf16[512,1024]{1,0:T(8,128)(2,1)} collective-permute-done((bf16[512,1024]{1,0:T(8,128)(2,1)}, bf16[512,1024]{1,0:T(8,128)(2,1)}, u32[]{:S(2)}, u32[]{:S(2)}) %collective-permute-start.3) | collective-permute-done | bytes 1048608 | tf_op jit(solution)/shard_map/ppermute | solution.py:11
  175.6 2.8 collective-permute-start.4
  178.4 10.2 %collective-permute-done.7 = bf16[64,512]{0,1:T(8,128)(2,1)S(1)} collective-permute-done((bf16[64,512]{0,1:T(8,128)(2,1)S(1)}, bf16[64,512]{0,1:T(8,128)(2,1)S(1)}, u32[]{:S(2)}, u32[]{:S(2)}) %collective-permute-start.7) | collective-permute-done | bytes 65568 | tf_op jit(solution)/shard_map/ppermute | solution.py:11
  190.0 4.7 %collective-permute-done.8 = bf16[64,512]{0,1:T(8,128)(2,1)S(1)} collective-permute-done((bf16[64,512]{0,1:T(8,128)(2,1)S(1)}, bf16[64,512]{0,1:T(8,128)(2,1)S(1)}, u32[]{:S(2)}, u32[]{:S(2)}) %collective-permute-start.8) | collective-permute-done | bytes 65568 | tf_op jit(solution)/shard_map/ppermute | solution.py:11
  194.7 4.5 %collective-permute-start.9 = (bf16[64,512]{0,1:T(8,128)(2,1)S(1)}, bf16[64,512]{0,1:T(8,128)(2,1)S(1)}, u32[]{:S(2)}, u32[]{:S(2)}) collective-permute-start(bf16[64,512]{0,1:T(8,128)(2,1)S(1)} %collective-permute-done.8), channel_id=1, source_target_pairs={{0,64},{1,65},{2,66},{3,67},{4,68},{5,69},{6,70},{7,71},{8,72},{9,... | collective-permute-start | bytes 196616 | tf_op jit(solution)/shard_map/ppermute | solution.py:11
  204.3 3.5 collective-permute-done.10
  207.8 4.2 %collective-permute-start.11 = (bf16[64,512]{0,1:T(8,128)(2,1)S(1)}, bf16[64,512]{0,1:T(8,128)(2,1)S(1)}, u32[]{:S(2)}, u32[]{:S(2)}) collective-permute-start(bf16[64,512]{0,1:T(8,128)(2,1)S(1)} %collective-permute-done.10), channel_id=1, source_target_pairs={{0,128},{1,129},{2,130},{3,131},{4,132},{5,133},{6,134},{7,135},{8... | collective-permute-start | bytes 196616 | tf_op jit(solution)/shard_map/ppermute | solution.py:11
  212.0 6.5 %fusion.26 = bf16[512,1024]{1,0:T(8,128)(2,1)} fusion(bf16[2,1024,1024]{2,1,0:T(8,128)(2,1)} %param.24, bf16[2,1024,1024]{2,1,0:T(8,128)(2,1)} %param.23, f32[512,1024]{1,0:T(8,128)} %get-tuple-element.12, f32[512]{0:T(512)S(1)} %add_rsqrt_fusion.3, f32[1024]{0:T(1024)S(1)} %bitcast.162), kind=kOutput, calls=%fused_computation.52 | convolution fusion | flops 2152202240 | bytes 7346176 | tf_op jit(solution)/shard_map/dot_general | solution.py:86
  219.9 7.6 %collective-permute-done.5 = bf16[512,1024]{1,0:T(8,128)(2,1)} collective-permute-done((bf16[512,1024]{1,0:T(8,128)(2,1)}, bf16[512,1024]{1,0:T(8,128)(2,1)}, u32[]{:S(2)}, u32[]{:S(2)}) %collective-permute-start.5) | collective-permute-done | bytes 1048608 | tf_op jit(solution)/shard_map/ppermute | solution.py:11
  231.5 7.3 %fusion.1 = (bf16[512,1024]{1,0:T(8,128)(2,1)S(1)}, bf16[512,1024]{1,0:T(8,128)(2,1)}) fusion(f32[512,1024]{1,0:T(8,128)} %get-tuple-element.12, bf16[512,1024]{1,0:T(8,128)(2,1)} %fusion.26, bf16[2,1024,1024]{2,1,0:T(8,128)(2,1)} %param.24, bf16[2,1024,1024]{2,1,0:T(8,128)(2,1)} %param.23, f32[512,1024]{1,0:T(8,128)} %get-tuple-element.10, ...), kind=kOutput, calls=%fused_computation.10 | convolution fusion | flops 2154823680 | bytes 11540480 | tf_op jit(solution)/shard_map/dot_general | solution.py:86
  239.5 86.9 %all_to_all.10 = bf16[32,64,512]{2,1,0:T(8,128)(2,1)S(1)} all-to-all(bf16[32,64,512]{2,1,0:T(8,128)(2,1)S(1)} %broadcast_in_dim.48), channel_id=1, replica_groups=mesh['src'=32,'tgt'=8] {'src'}, dimensions={0} | all-to-all | bytes 4194304 | tf_op jit(solution)/shard_map/all_to_all | solution.py:16
  326.4 2.5 copy.27
  328.9 4.3 %reshape_reshape.7 = bf16[64,128,128]{2,1,0:T(8,128)(2,1)} reshape(bf16[64,32,512]{2,1,0:T(8,128)(2,1)} %copy.27) | data formatting | bytes 4194304 | tf_op jit(solution)/shard_map/reshape;reshape | solution.py:67
  333.2 4.3 %copy.28 = bf16[64,128,128]{2,0,1:T(8,128)(2,1)} copy(bf16[64,128,128]{2,1,0:T(8,128)(2,1)} %reshape_reshape.7) | data formatting | bytes 4194304 | tf_op jit(solution)/shard_map/reshape;reshape | solution.py:67
  341.6 2.8 collective-permute-done.12
  344.3 2.4 collective-permute-start.13
  349.1 2.4 collective-permute-start.14
  353.8 9.7 %collective-permute-start.15 = (bf16[64,512]{0,1:T(8,128)(2,1)S(1)}, bf16[64,512]{0,1:T(8,128)(2,1)S(1)}, u32[]{:S(2)}, u32[]{:S(2)}) collective-permute-start(bf16[64,512]{0,1:T(8,128)(2,1)S(1)} %collective-permute-done.14), channel_id=1, source_target_pairs={{0,64},{1,65},{2,66},{3,67},{4,68},{5,69},{6,70},{7,71},{8,72},{9,... | collective-permute-start | bytes 196616 | tf_op jit(solution)/shard_map/ppermute | solution.py:11
  366.6 4.8 %collective-permute-done.16 = bf16[64,512]{0,1:T(8,128)(2,1)S(1)} collective-permute-done((bf16[64,512]{0,1:T(8,128)(2,1)S(1)}, bf16[64,512]{0,1:T(8,128)(2,1)S(1)}, u32[]{:S(2)}, u32[]{:S(2)}) %collective-permute-start.16) | collective-permute-done | bytes 65568 | tf_op jit(solution)/shard_map/ppermute | solution.py:11
  371.6 6.6 %fusion.32 = bf16[512,1024]{1,0:T(8,128)(2,1)} fusion(bf16[2,1024,1024]{2,1,0:T(8,128)(2,1)} %param.24, bf16[2,1024,1024]{2,1,0:T(8,128)(2,1)} %param.23, f32[512,1024]{1,0:T(8,128)} %get-tuple-element.16, f32[512]{0:T(512)S(1)} %add_rsqrt_fusion.1, f32[1024]{0:T(1024)S(1)} %bitcast.160), kind=kOutput, calls=%fused_computation.54 | convolution fusion | flops 2152202240 | bytes 7346176 | tf_op jit(solution)/shard_map/dot_general | solution.py:86
  379.5 3.9 multiply_reduce_fusion
  383.4 7.2 %fusion.41 = bf16[1,1,512,1024]{3,2,1,0:T(8,128)(2,1)} fusion(bf16[2,1024,1024]{2,1,0:T(8,128)(2,1)} %param.24, f32[512,1024]{1,0:T(8,128)} %get-tuple-element.16, bf16[512,1024]{1,0:T(8,128)(2,1)} %fusion.32, bf16[2,1024,1024]{2,1,0:T(8,128)(2,1)} %param.23, f32[512,1024]{1,0:T(8,128)} %get-tuple-element.18, f32[512]{0:T(512)S(1)} %add_rsqrt_fusion, ...), kind=kOutput, calls=%fused_computation.63 | convolution fusion | flops 2154823680 | bytes 10491904 | tf_op jit(solution)/shard_map/dot_general | solution.py:86
  (83 shorter events, 36.6 us)
Async XLA Ops:
  0.0 155.7 %copy-start = (bf16[1,1,16,128,128]{4,3,2,1,0:T(8,128)(2,1)S(1)}, bf16[1,1,16,128,128]{4,3,2,1,0:T(8,128)(2,1)}, u32[]{:S(2)}) copy-start(bf16[1,1,16,128,128]{4,3,2,1,0:T(8,128)(2,1)} %param.16) | copy-start | bytes 1572868
  3.3 13.0 %copy-start.1 = (bf16[1,1,512,1024]{3,2,1,0:T(8,128)(2,1)S(1)}, bf16[1,1,512,1024]{3,2,1,0:T(8,128)(2,1)}, u32[]{:S(2)}) copy-start(bf16[1,1,512,1024]{3,2,1,0:T(8,128)(2,1)} %param.15) | copy-start | bytes 3145732
  3.3 137.5 %all-to-all-start = ((bf16[32,64,512]{2,1,0:T(8,128)(2,1)}), bf16[32,64,512]{2,1,0:T(8,128)(2,1)}, u32[]{:S(2)}, u32[]{:S(2)}) async-start(bf16[32,64,512]{2,1,0:T(8,128)(2,1)} %broadcast_in_dim.45), calls=%async_computation | async-start | bytes 4194304 | tf_op jit(solution)/shard_map/all_to_all | solution.py:16
  16.3 96.3 %copy-start.10 = (s32[1,1,16]{2,1,0:T(1,128)S(1)}, s32[1,1,16]{2,1,0:T(1,128)}, u32[]{:S(2)}) copy-start(s32[1,1,16]{2,1,0:T(1,128)} %param.18) | copy-start | bytes 196
  16.3 96.3 %copy-start.7 = (s32[1,1,512]{2,1,0:T(1,128)S(1)}, s32[1,1,512]{2,1,0:T(1,128)}, u32[]{:S(2)}) copy-start(s32[1,1,512]{2,1,0:T(1,128)} %param.20) | copy-start | bytes 6148
  16.3 124.5 %copy-start.8 = (f32[2,1024]{1,0:T(2,128)S(1)}, f32[2,1024]{1,0:T(2,128)}, u32[]{:S(2)}) copy-start(f32[2,1024]{1,0:T(2,128)} %param.25) | copy-start | bytes 24580
  16.3 44.3 %collective-permute-start = (bf16[512,1024]{1,0:T(8,128)(2,1)S(1)}, bf16[512,1024]{1,0:T(8,128)(2,1)S(1)}, u32[]{:S(2)}, u32[]{:S(2)}) collective-permute-start(bf16[512,1024]{1,0:T(8,128)(2,1)S(1)} %bitcast.149), channel_id=1, source_target_pairs={{0,1},{1,0},{2,3},{3,2},{4,5},{5,4},{6,7},{7,6},{8,9},{9,8},{10,11... | collective-permute-start | bytes 3145736 | tf_op jit(solution)/shard_map/ppermute | solution.py:11
  60.7 50.5 %collective-permute-start.1 = (bf16[512,1024]{1,0:T(8,128)(2,1)S(1)}, bf16[512,1024]{1,0:T(8,128)(2,1)}, u32[]{:S(2)}, u32[]{:S(2)}) collective-permute-start(bf16[512,1024]{1,0:T(8,128)(2,1)S(1)} %collective-permute-done), channel_id=1, source_target_pairs={{0,32},{1,33},{2,34},{3,35},{4,36},{5,37},{6,38},{7,39},{8,40},{9,... | collective-permute-start | bytes 3145736 | tf_op jit(solution)/shard_map/ppermute | solution.py:11
  111.3 24.3 %collective-permute-start.2 = (bf16[512,1024]{1,0:T(8,128)(2,1)S(1)}, bf16[512,1024]{1,0:T(8,128)(2,1)}, u32[]{:S(2)}, u32[]{:S(2)}) collective-permute-start(bf16[512,1024]{1,0:T(8,128)(2,1)S(1)} %broadcast_select_fusion), channel_id=1, source_target_pairs={{0,2},{1,3},{2,0},{3,1},{4,6},{5,7},{6,4},{7,5},{8,10},{9,11},{10,... | collective-permute-start | bytes 3145736 | tf_op jit(solution)/shard_map/ppermute | solution.py:11
  135.6 39.9 %collective-permute-start.3 = (bf16[512,1024]{1,0:T(8,128)(2,1)}, bf16[512,1024]{1,0:T(8,128)(2,1)}, u32[]{:S(2)}, u32[]{:S(2)}) collective-permute-start(bf16[512,1024]{1,0:T(8,128)(2,1)} %collective-permute-done.2), channel_id=1, source_target_pairs={{0,64},{1,65},{2,66},{3,67},{4,68},{5,69},{6,70},{7,71},{8,72},{9,... | collective-permute-start | bytes 3145736 | tf_op jit(solution)/shard_map/ppermute | solution.py:11
  149.3 6.8 %copy-start.9 = (s32[1,1,16]{2,1,0:T(1,128)S(1)}, s32[1,1,16]{2,1,0:T(1,128)}, u32[]{:S(2)}) copy-start(s32[1,1,16]{2,1,0:T(1,128)} %param.17) | copy-start | bytes 196
  156.1 43.1 %copy-start.5 = (bf16[2,64,1024]{2,1,0:T(8,128)(2,1)S(1)}, bf16[2,64,1024]{2,1,0:T(8,128)(2,1)}, u32[]{:S(2)}) copy-start(bf16[2,64,1024]{2,1,0:T(8,128)(2,1)} %param.22) | copy-start | bytes 786436
  156.5 5.1 %collective-permute-start.6 = (bf16[64,512]{0,1:T(8,128)(2,1)S(1)}, bf16[64,512]{0,1:T(8,128)(2,1)S(1)}, u32[]{:S(2)}, u32[]{:S(2)}) collective-permute-start(bf16[64,512]{0,1:T(8,128)(2,1)S(1)} %copy.25), channel_id=1, source_target_pairs={{0,1},{1,0},{2,3},{3,2},{4,5},{5,4},{6,7},{7,6},{8,9},{9,8},{10,11... | collective-permute-start | bytes 196616 | tf_op jit(solution)/shard_map/ppermute | solution.py:11
  161.6 27.0 %collective-permute-start.7 = (bf16[64,512]{0,1:T(8,128)(2,1)S(1)}, bf16[64,512]{0,1:T(8,128)(2,1)S(1)}, u32[]{:S(2)}, u32[]{:S(2)}) collective-permute-start(bf16[64,512]{0,1:T(8,128)(2,1)S(1)} %collective-permute-done.6), channel_id=1, source_target_pairs={{0,32},{1,33},{2,34},{3,35},{4,36},{5,37},{6,38},{7,39},{8,40},{9,... | collective-permute-start | bytes 196616 | tf_op jit(solution)/shard_map/ppermute | solution.py:11
  175.6 25.3 %copy-start.2 = (bf16[512,1024]{1,0:T(8,128)(2,1)}, bf16[512,1024]{1,0:T(8,128)(2,1)S(1)}, u32[]{:S(2)}) copy-start(bf16[512,1024]{1,0:T(8,128)(2,1)S(1)} %broadcast_select_fusion.1) | copy-start | bytes 3145732
  175.6 36.4 %collective-permute-start.4 = (bf16[512,1024]{1,0:T(8,128)(2,1)S(1)}, bf16[512,1024]{1,0:T(8,128)(2,1)}, u32[]{:S(2)}, u32[]{:S(2)}) collective-permute-start(bf16[512,1024]{1,0:T(8,128)(2,1)S(1)} %broadcast_select_fusion.1), channel_id=1, source_target_pairs={{0,4},{1,5},{2,6},{3,7},{4,0},{5,1},{6,2},{7,3},{8,12},{9,13},{10,... | collective-permute-start | bytes 3145736 | tf_op jit(solution)/shard_map/ppermute | solution.py:11
  188.7 6.0 %collective-permute-start.8 = (bf16[64,512]{0,1:T(8,128)(2,1)S(1)}, bf16[64,512]{0,1:T(8,128)(2,1)S(1)}, u32[]{:S(2)}, u32[]{:S(2)}) collective-permute-start(bf16[64,512]{0,1:T(8,128)(2,1)S(1)} %broadcast_select_fusion.4), channel_id=1, source_target_pairs={{0,2},{1,3},{2,0},{3,1},{4,6},{5,7},{6,4},{7,5},{8,10},{9,11},{10,... | collective-permute-start | bytes 196616 | tf_op jit(solution)/shard_map/ppermute | solution.py:11
  194.7 7.7 %collective-permute-start.9 = (bf16[64,512]{0,1:T(8,128)(2,1)S(1)}, bf16[64,512]{0,1:T(8,128)(2,1)S(1)}, u32[]{:S(2)}, u32[]{:S(2)}) collective-permute-start(bf16[64,512]{0,1:T(8,128)(2,1)S(1)} %collective-permute-done.8), channel_id=1, source_target_pairs={{0,64},{1,65},{2,66},{3,67},{4,68},{5,69},{6,70},{7,71},{8,72},{9,... | collective-permute-start | bytes 196616 | tf_op jit(solution)/shard_map/ppermute | solution.py:11
  202.4 5.4 %collective-permute-start.10 = (bf16[64,512]{0,1:T(8,128)(2,1)S(1)}, bf16[64,512]{0,1:T(8,128)(2,1)S(1)}, u32[]{:S(2)}, u32[]{:S(2)}) collective-permute-start(bf16[64,512]{0,1:T(8,128)(2,1)S(1)} %broadcast_select_fusion.6), channel_id=1, source_target_pairs={{0,4},{1,5},{2,6},{3,7},{4,0},{5,1},{6,2},{7,3},{8,12},{9,13},{10,... | collective-permute-start | bytes 196616 | tf_op jit(solution)/shard_map/ppermute | solution.py:11
  207.8 10.7 %collective-permute-start.11 = (bf16[64,512]{0,1:T(8,128)(2,1)S(1)}, bf16[64,512]{0,1:T(8,128)(2,1)S(1)}, u32[]{:S(2)}, u32[]{:S(2)}) collective-permute-start(bf16[64,512]{0,1:T(8,128)(2,1)S(1)} %collective-permute-done.10), channel_id=1, source_target_pairs={{0,128},{1,129},{2,130},{3,131},{4,132},{5,133},{6,134},{7,135},{8... | collective-permute-start | bytes 196616 | tf_op jit(solution)/shard_map/ppermute | solution.py:11
  212.0 15.5 %collective-permute-start.5 = (bf16[512,1024]{1,0:T(8,128)(2,1)}, bf16[512,1024]{1,0:T(8,128)(2,1)}, u32[]{:S(2)}, u32[]{:S(2)}) collective-permute-start(bf16[512,1024]{1,0:T(8,128)(2,1)} %collective-permute-done.4), channel_id=1, source_target_pairs={{0,128},{1,129},{2,130},{3,131},{4,132},{5,133},{6,134},{7,135},{8... | collective-permute-start | bytes 3145736 | tf_op jit(solution)/shard_map/ppermute | solution.py:11
  212.0 15.5 %copy-start.3 = (bf16[512,1024]{1,0:T(8,128)(2,1)S(1)}, bf16[512,1024]{1,0:T(8,128)(2,1)}, u32[]{:S(2)}) copy-start(bf16[512,1024]{1,0:T(8,128)(2,1)} %copy-done.2) | copy-start | bytes 3145732
  231.5 7.3 %copy-start.6 = (bf16[2,1024,64]{1,2,0:T(8,128)(2,1)S(1)}, bf16[2,1024,64]{1,2,0:T(8,128)(2,1)}, u32[]{:S(2)}) copy-start(bf16[2,1024,64]{1,2,0:T(8,128)(2,1)} %param.21) | copy-start | bytes 786436
  340.4 3.9 collective-permute-start.12
  344.3 4.7 %collective-permute-start.13 = (bf16[64,512]{0,1:T(8,128)(2,1)S(1)}, bf16[64,512]{0,1:T(8,128)(2,1)S(1)}, u32[]{:S(2)}, u32[]{:S(2)}) collective-permute-start(bf16[64,512]{0,1:T(8,128)(2,1)S(1)} %collective-permute-done.12), channel_id=1, source_target_pairs={{0,32},{1,33},{2,34},{3,35},{4,36},{5,37},{6,38},{7,39},{8,40},{9,... | collective-permute-start | bytes 196616 | tf_op jit(solution)/shard_map/ppermute | solution.py:11
  349.1 4.8 %collective-permute-start.14 = (bf16[64,512]{0,1:T(8,128)(2,1)S(1)}, bf16[64,512]{0,1:T(8,128)(2,1)S(1)}, u32[]{:S(2)}, u32[]{:S(2)}) collective-permute-start(bf16[64,512]{0,1:T(8,128)(2,1)S(1)} %broadcast_select_fusion.3), channel_id=1, source_target_pairs={{0,2},{1,3},{2,0},{3,1},{4,6},{5,7},{6,4},{7,5},{8,10},{9,11},{10,... | collective-permute-start | bytes 196616 | tf_op jit(solution)/shard_map/ppermute | solution.py:11
  353.8 12.1 %collective-permute-start.15 = (bf16[64,512]{0,1:T(8,128)(2,1)S(1)}, bf16[64,512]{0,1:T(8,128)(2,1)S(1)}, u32[]{:S(2)}, u32[]{:S(2)}) collective-permute-start(bf16[64,512]{0,1:T(8,128)(2,1)S(1)} %collective-permute-done.14), channel_id=1, source_target_pairs={{0,64},{1,65},{2,66},{3,67},{4,68},{5,69},{6,70},{7,71},{8,72},{9,... | collective-permute-start | bytes 196616 | tf_op jit(solution)/shard_map/ppermute | solution.py:11
  366.0 5.4 %collective-permute-start.16 = (bf16[64,512]{0,1:T(8,128)(2,1)S(1)}, bf16[64,512]{0,1:T(8,128)(2,1)S(1)}, u32[]{:S(2)}, u32[]{:S(2)}) collective-permute-start(bf16[64,512]{0,1:T(8,128)(2,1)S(1)} %broadcast_select_fusion.5), channel_id=1, source_target_pairs={{0,4},{1,5},{2,6},{3,7},{4,0},{5,1},{6,2},{7,3},{8,12},{9,13},{10,... | collective-permute-start | bytes 196616 | tf_op jit(solution)/shard_map/ppermute | solution.py:11
  371.4 6.8 %collective-permute-start.17 = (bf16[64,512]{0,1:T(8,128)(2,1)S(1)}, bf16[64,512]{0,1:T(8,128)(2,1)S(1)}, u32[]{:S(2)}, u32[]{:S(2)}) collective-permute-start(bf16[64,512]{0,1:T(8,128)(2,1)S(1)} %collective-permute-done.16), channel_id=1, source_target_pairs={{0,128},{1,129},{2,130},{3,131},{4,132},{5,133},{6,134},{7,135},{8... | collective-permute-start | bytes 196616 | tf_op jit(solution)/shard_map/ppermute | solution.py:11
  371.6 8.0 %copy-start.4 = (bf16[512,1024]{1,0:T(8,128)(2,1)S(1)}, bf16[512,1024]{1,0:T(8,128)(2,1)}, u32[]{:S(2)}) copy-start(bf16[512,1024]{1,0:T(8,128)(2,1)} %fusion.26) | copy-start | bytes 3145732
where the time goes:
time: 396 us; the launch traced here: 391 us
  waiting for transfers between devices  170 us (43%)
  blocking collectives  86.9 us (22%)
  starting transfers between devices  57.5 us (15%)
  matrix products  40.2 us (10%)
  local copies, waits for them, and re-layouts  35 us (9%)
    ppermute x18, waiting for transfers between devices, partner(): lax.ppermute(value, axis, [(i, i ^ 1 << bit) for i in range(lax.axis_size...  170 us
    all_to_all x1, blocking collectives, from_everyone(): return lax.all_to_all(copies, axis, split_axis=0, concat_axis=0, tiled=True)  86.9 us
    ppermute x18, starting transfers between devices, partner(): lax.ppermute(value, axis, [(i, i ^ 1 << bit) for i in range(lax.axis_size...  44.6 us
    dot_general x4, matrix products, transform(): jnp.dot(activated, w_out_l, preferred_element_type=jnp.float32)  27.6 us
    another operation x4, local copies, waits for them, and re-layouts, triplet_sums(): blocks = pooled.reshape(width, pooled.shape[1] // BLK, BLK)  17.2 us
    all_to_all x1, starting transfers between devices, from_everyone(): return lax.all_to_all(copies, axis, split_axis=0, concat_axis=0, tiled=True)  12.9 us
    dot_general x4, matrix products, transform(): jnp.einsum('ce,cd->ed', agg_low, w_up_l, preferred_element_type=jnp.float32)  9.26 us
  transfers between devices with their start and end apart: 19, of which 15 were waited for; matrix products, arithmetic and copies ran while one was open for 9% of the time, Pallas kernels for 0%

commit v1 on v0

v1 whole, which is shorter than its diff:
```python
import functools

import jax
import jax.numpy as jnp
from jax import lax
from jax.experimental import pallas as pl
from jax.experimental.pallas import tpu as pltpu
from jax.sharding import PartitionSpec as P

MESH = pl.DeviceIdType.MESH
BF16 = jnp.bfloat16
F32 = jnp.float32
D = 1024
E = 512
T = 64
BLK = 128
NB = 16
SUB = 2
NBLK = 128


def place():
    s = lax.axis_index("src")
    t = lax.axis_index("tgt")
    return dict(y1=s // 16, z=(s // 2) % 8, c=s % 2, x=t // 2, y0=t % 2)


def device(x, y1, y0, z, c):
    return (y1 * 16 + z * 2 + c, x * 2 + y0)


def kernel(
    tgt_s, src_s, cnt_s, st_h, coef_h, rs_ref, wp_h, wup_h, win_h, wout_h, gain_ref, out_ref,
    st, coef, wp, wup, win, wout, g0, g1, l1, l2, fin, perm, lhs, aggt, aggm, pbt, pbm,
    summed, branch, mst, msum, mbr, nrm, act, lsem,
    gs, yr, zr, sr, l1s, l1r, l2s, l2r, l3s, l3r, ms, mr,
):
    k = place()
    x, y1, y0, z, c = k["x"], k["y1"], k["y0"], k["z"], k["c"]
    z2, z1, z0 = z // 4, (z // 2) % 2, z % 2
    x1, x0 = x // 2, x % 2
    me_slot = y1 * 16 + z * 2 + c

    sib = device(x, y1, y0, z, 1 - c)
    ypart = device(x, 1 - y1, y0, z, c)
    zup = device(x, y1, y0, (z + 1) % 8, c)
    zdn = device(x, y1, y0, (z + 7) % 8, c)
    mirror = device(y1 * 2 + z2, x1, z1, x0 * 4 + y0 * 2 + z0, c)
    diag = (x1 == y1) & (x0 == z2) & (y0 == z1)
    not_diag = jnp.logical_not(diag)

    def leg2(s):
        s1, s0 = s // 2, s % 2
        dest = device(x, s1, z1, s0 * 4 + y0 * 2 + z0, c)
        own = (y1 == s1) & (y0 == z1) & (z2 == s0)
        return dest, own

    xs = [(x + i) % 4 for i in range(1, 4)]

    bar = pltpu.get_barrier_semaphore()

    def signal(d):
        pl.semaphore_signal(bar, inc=1, device_id=d, device_id_type=MESH)

    @pl.when(not_diag)
    def _():
        signal(mirror)

    for s in range(4):
        dest, own = leg2(s)

        @pl.when(jnp.logical_not(own))
        def _(dest=dest):
            signal(dest)

    for d in (ypart, zup, zdn, sib):
        signal(d)
    for xx in xs:
        signal(device(xx, y1, y0, z, c))

    loads = [
        pltpu.make_async_copy(a, b, lsem.at[i])
        for i, (a, b) in enumerate(
            [(st_h, st), (wp_h, wp), (coef_h, coef), (wup_h, wup), (win_h.at[0], win.at[0]),
             (wout_h.at[0], wout.at[0]), (win_h.at[1], win.at[1]), (wout_h.at[1], wout.at[1])]
        )
    ]
    for cp in loads:
        cp.start()

    loads[0].wait()
    loads[1].wait()

    def proj_t(l, rows):
        return lax.dot_general(
            wp[l], rows, (((1,), (1,)), ((), ())), preferred_element_type=F32
        )

    def put_own(g, val):
        for b in range(4):
            g[me_slot * 4 + b] = val[:, b * BLK : (b + 1) * BLK].astype(BF16)

    put_own(g0, proj_t(0, st[...]))

    n_own2 = (y0 == z1).astype(jnp.int32)
    pl.semaphore_wait(bar, 4 + 3 + 4 - n_own2 + not_diag.astype(jnp.int32))

    def remote(src, dst, ss, rs, d):
        return pltpu.make_async_remote_copy(
            src_ref=src, dst_ref=dst, send_sem=ss, recv_sem=rs, device_id=d, device_id_type=MESH
        )

    def make_gather(l, g):
        def piece(col, zz, lo=0, n=4):
            return g.at[pl.ds((col * 16 + zz * 2 + c) * 4 + lo, n)]

        def to_sib(p):
            remote(p, p, gs.at[l], sr.at[l], sib).start()

        def z_copy(p, direction, dist, b):
            return remote(
                p, p, gs.at[l], zr.at[l, direction, dist - 1, b], zup if direction == 0 else zdn
            )

        def part(direction, dist, b, at_dist):
            col = y1 if b == 0 else 1 - y1
            zz = (z + 8 - at_dist) % 8 if direction == 0 else (z + at_dist) % 8
            if dist == 4:
                return piece(col, zz, 0 if direction == 0 else 2, 2)
            return piece(col, zz)

        def start():
            own = piece(y1, z)
            for direction in (0, 1):
                z_copy(part(direction, 1, 0, 0), direction, 1, 0).start()
            remote(own, own, gs.at[l], yr.at[l], ypart).start()
            to_sib(own)

        def from_y():
            other = piece(1 - y1, z)
            remote(other, other, gs.at[l], yr.at[l], ypart).wait_recv()
            for direction in (0, 1):
                z_copy(part(direction, 1, 1, 0), direction, 1, 1).start()
            to_sib(other)

        def step(dist, b):
            for direction in (0, 1):
                got = part(direction, dist, b, dist)
                z_copy(got, direction, dist, b).wait_recv()
                if dist < 4:
                    z_copy(part(direction, dist + 1, b, dist), direction, dist + 1, b).start()
                to_sib(got)

        def finish():
            half = g.at[pl.ds(0, 64)]
            remote(half, half, gs.at[l], sr.at[l], sib).wait_recv()

        def drain():
            a = g.at[pl.ds(0, 4 * 31)]
            remote(a, a, gs.at[l], sr.at[l], sib).wait_send()

        return start, from_y, step, finish, drain

    gat0 = make_gather(0, g0)
    gat1 = make_gather(1, g1)
    gat0[0]()

    rows_sub = BLK // SUB

    def sub(ref, slot, j):
        return ref.at[slot, pl.ds(j * rows_sub, rows_sub)]

    def st_sub(chunk, j):
        return st.at[pl.ds(chunk * BLK + j * rows_sub, rows_sub)]

    def leg1_start(j):
        for i, xx in enumerate(xs):
            remote(
                st_sub(xx, j), sub(l1, x, j), l1s.at[j], l1r.at[j, 3 - 1 - i], device(xx, y1, y0, z, c)
            ).start()
        pltpu.make_async_copy(st_sub(x, j), sub(l1, x, j), l1r.at[j, 3]).start()

    def leg1_wait(j):
        for i, xx in enumerate(xs):
            remote(st_sub(xx, j), sub(l1, xx, j), l1s.at[j], l1r.at[j, i], sib).wait_recv()
        pltpu.make_async_copy(st_sub(x, j), sub(l1, x, j), l1r.at[j, 3]).wait()

    def leg2_start(j):
        for s in range(4):
            dest, own = leg2(s)
            there = y1 * 2 + z2

            @pl.when(jnp.logical_not(own))
            def _(dest=dest, s=s):
                remote(
                    sub(l1, s, j), sub(l2, there, j), l2s.at[j], l2r.at[j, there], dest
                ).start()

            @pl.when(own)
            def _(s=s):
                pltpu.make_async_copy(sub(l1, s, j), sub(l2, s, j), l2r.at[j, s]).start()

    def leg2_wait(j):
        for s in range(4):
            dest, own = leg2(s)

            @pl.when(jnp.logical_not(own))
            def _(s=s, dest=dest):
                remote(sub(l1, s, j), sub(l2, s, j), l2s.at[j], l2r.at[j, s], dest).wait_recv()

            @pl.when(own)
            def _(s=s):
                pltpu.make_async_copy(sub(l1, s, j), sub(l2, s, j), l2r.at[j, s]).wait()

    def fin_sub(chunk, j):
        return fin.at[pl.ds(chunk * BLK + j * rows_sub, rows_sub)]

    def leg3_start(j):
        for i, xx in enumerate(xs):
            remote(
                sub(l2, xx, j), fin_sub(x, j), l3s.at[j], l3r.at[j, 3 - 1 - i], device(xx, y1, y0, z, c)
            ).start()
        pltpu.make_async_copy(sub(l2, x, j), fin_sub(x, j), l3r.at[j, 3]).start()

    def leg3_wait(j):
        for i, xx in enumerate(xs):
            remote(sub(l2, xx, j), fin_sub(xx, j), l3s.at[j], l3r.at[j, i], sib).wait_recv()
        pltpu.make_async_copy(sub(l2, x, j), fin_sub(x, j), l3r.at[j, 3]).wait()

    def legs_drain():
        for j in range(SUB):
            rows = pl.ds(0, rows_sub)
            three, four = l1.at[pl.ds(0, 3), rows], l1.at[pl.ds(0, 4), rows]
            remote(three, three, l1s.at[j], l1r.at[j, 0], sib).wait_send()
            remote(three, three, l3s.at[j], l3r.at[j, 0], sib).wait_send()

            @pl.when(y0 == z1)
            def _(j=j, three=three):
                remote(three, three, l2s.at[j], l2r.at[j, 0], sib).wait_send()

            @pl.when(y0 != z1)
            def _(j=j, four=four):
                remote(four, four, l2s.at[j], l2r.at[j, 0], sib).wait_send()

    def swap_start(i, src, dst):
        @pl.when(not_diag)
        def _():
            remote(src, dst, ms.at[i], mr.at[i], mirror).start()

        @pl.when(diag)
        def _():
            pltpu.make_async_copy(src, dst, mr.at[i]).start()

    def swap_wait(i, src, dst):
        @pl.when(not_diag)
        def _():
            remote(src, dst, ms.at[i], mr.at[i], mirror).wait_recv()

        @pl.when(diag)
        def _():
            pltpu.make_async_copy(src, dst, mr.at[i]).wait()

    def swap_drain(i, src, dst):
        @pl.when(not_diag)
        def _():
            remote(src, dst, ms.at[i], mr.at[i], mirror).wait_send()

    def triplets(g, out):
        live = cnt_s[0]
        zero = jnp.zeros((T, BLK), BF16)
        for b in range(NB):
            blk = g[src_s[b]]
            tb = jnp.where(b < live, tgt_s[b], -1)
            for o in range(4):
                lhs[o * T : (o + 1) * T, b * BLK : (b + 1) * BLK] = jnp.where(tb == o, blk, zero)
        acc = jnp.dot(lhs[...], coef[...].reshape(NB * BLK, BLK), preferred_element_type=F32)
        for o in range(4):
            out[:, o * BLK : (o + 1) * BLK] = acc[o * T : (o + 1) * T].astype(BF16)

    def permute_t(val):
        return jnp.dot(val, perm[...], preferred_element_type=F32)

    def norm(l, rows_ref, agg, sum_ref):
        def body(r, _):
            rows = pl.ds(pl.multiple_of(r * BLK, BLK), BLK)
            up = lax.dot_general(
                agg[:, rows], wup[l], (((0,), (0,)), ((), ())), preferred_element_type=F32
            )
            s = rows_ref[rows, :].astype(F32) + up
            sum_ref[rows, :] = s
            scale = lax.rsqrt(jnp.mean(s * s, axis=-1, keepdims=True) + 1e-06)
            nrm[rows, :] = (gain_ref[l : l + 1, :] * s * scale).astype(BF16)
            return 0

        lax.fori_loop(0, 4, body, 0)

    def hidden(l):
        def body(n, _):
            cols = pl.ds(pl.multiple_of(n * 256, 256), 256)
            h = jnp.dot(nrm[...], win[l, :, cols], preferred_element_type=F32)
            act[:, cols] = (h / (1.0 + jnp.exp(-h))).astype(BF16)
            return 0

        lax.fori_loop(0, 4, body, 0)

    def outer(l, br):
        def body(n, _):
            cols = pl.ds(pl.multiple_of(n * 256, 256), 256)
            br[:, cols] = jnp.dot(
                act[...], wout[l, :, cols], preferred_element_type=F32
            ).astype(BF16)
            return 0

        lax.fori_loop(0, 4, body, 0)

    def by_rows(f):
        def body(r, _):
            f(pl.ds(pl.multiple_of(r * BLK, BLK), BLK))
            return 0

        lax.fori_loop(0, 4, body, 0)

    for j in range(SUB):
        leg1_start(j)

    def onehot(rows, r):
        ids = lax.broadcasted_iota(jnp.int32, (BLK, E), 0) + r * BLK
        perm[rows, :] = jnp.where(ids == rs_ref[0:1, :], 1.0, 0.0).astype(BF16)

    def onehot_body(r, _):
        onehot(pl.ds(pl.multiple_of(r * BLK, BLK), BLK), r)
        return 0

    lax.fori_loop(0, 4, onehot_body, 0)

    start, from_y, step, finish, drain0 = gat0
    step(1, 0)
    from_y()
    step(1, 1)
    step(2, 0)
    leg1_wait(0)
    step(2, 1)
    step(3, 0)
    leg2_start(0)
    step(3, 1)
    step(4, 0)
    step(4, 1)
    leg1_wait(1)
    leg2_start(1)
    finish()

    loads[2].wait()
    triplets(g0, aggt.at[0])
    swap_start(0, aggt.at[0], aggm.at[0])
    for i in (3, 4, 5):
        loads[i].wait()
    norm(0, st, aggt.at[0], summed)
    hidden(0)
    outer(0, branch)
    pbt[...] = proj_t(1, branch[...]).astype(BF16)
    swap_start(1, pbt, pbm)

    def part_sum(rows):
        nrm[rows, :] = (summed[rows, :] + branch[rows, :].astype(F32)).astype(BF16)

    by_rows(part_sum)
    half1 = proj_t(1, nrm[...])
    swap_wait(1, pbt, pbm)
    put_own(g1, half1 + permute_t(pbm[...]))
    start, from_y, step, finish, drain1 = gat1
    start()
    leg2_wait(0)
    leg3_start(0)
    step(1, 0)
    from_y()
    step(1, 1)
    step(2, 0)
    step(2, 1)
    step(3, 0)
    step(3, 1)
    step(4, 0)
    step(4, 1)
    leg2_wait(1)
    leg3_start(1)
    finish()
    triplets(g1, aggt.at[1])
    swap_start(2, aggt.at[1], aggm.at[1])

    swap_wait(0, aggt.at[0], aggm.at[0])
    act[0:T, 0:E] = permute_t(aggm[0]).astype(BF16)
    aggm[0] = act[0:T, 0:E]
    leg3_wait(0)
    leg3_wait(1)

    def take_rows(n, _):
        cols = pl.ds(pl.multiple_of(n * 256, 256), 256)
        mst[:, cols] = lax.dot_general(
            perm[...], fin[:, cols], (((0,), (0,)), ((), ())), preferred_element_type=F32
        ).astype(BF16)
        return 0

    lax.fori_loop(0, 4, take_rows, 0)
    norm(0, mst, aggm.at[0], msum)
    hidden(0)
    outer(0, mbr)

    def next_state(rows):
        b = branch[rows, :].astype(F32)
        m = mbr[rows, :].astype(F32)
        st[rows, :] = ((summed[rows, :] + b) + m).astype(BF16)
        mst[rows, :] = ((msum[rows, :] + m) + b).astype(BF16)

    legs_drain()
    by_rows(next_state)

    for i in (6, 7):
        loads[i].wait()
    norm(1, st, aggt.at[1], summed)
    hidden(1)
    outer(1, branch)
    swap_wait(2, aggt.at[1], aggm.at[1])
    act[0:T, 0:E] = permute_t(aggm[1]).astype(BF16)
    aggm[1] = act[0:T, 0:E]
    norm(1, mst, aggm.at[1], msum)
    hidden(1)
    outer(1, mbr)

    def final(rows):
        out_ref[rows, :] = (
            (summed[rows, :] + branch[rows, :].astype(F32)) + mbr[rows, :].astype(F32)
        ).astype(BF16)

    by_rows(final)

    drain0()
    drain1()
    swap_drain(0, aggt.at[0], aggm.at[0])
    swap_drain(1, pbt, pbm)
    swap_drain(2, aggt.at[1], aggm.at[1])


def local(
    edge_states, triplet_coeff, block_target, block_source, block_count, reverse_slot,
    w_proj, w_up, w_in, w_out, norm_gain,
):
    vmem = pl.BlockSpec(memory_space=pltpu.VMEM)
    smem = pl.BlockSpec(memory_space=pltpu.SMEM)
    hbm = pl.BlockSpec(memory_space=pl.ANY)
    dma = pltpu.SemaphoreType.DMA
    out = pl.pallas_call(
        kernel,
        out_shape=jax.ShapeDtypeStruct((E, D), BF16),
        in_specs=[smem, smem, smem, hbm, hbm, vmem, hbm, hbm, hbm, hbm, vmem],
        out_specs=vmem,
        scratch_shapes=[
            pltpu.VMEM((E, D), BF16),
            pltpu.VMEM((NB, BLK, BLK), BF16),
            pltpu.VMEM((2, T, D), BF16),
            pltpu.VMEM((2, T, D), BF16),
            pltpu.VMEM((2, D, D), BF16),
            pltpu.VMEM((2, D, D), BF16),
            pltpu.VMEM((NBLK, T, BLK), BF16),
            pltpu.VMEM((NBLK, T, BLK), BF16),
            pltpu.VMEM((4, BLK, D), BF16),
            pltpu.VMEM((4, BLK, D), BF16),
            pltpu.VMEM((E, D), BF16),
            pltpu.VMEM((E, E), BF16),
            pltpu.VMEM((4 * T, NB * BLK), BF16),
            pltpu.VMEM((2, T, E), BF16),
            pltpu.VMEM((2, T, E), BF16),
            pltpu.VMEM((T, E), BF16),
            pltpu.VMEM((T, E), BF16),
            pltpu.VMEM((E, D), F32),
            pltpu.VMEM((E, D), BF16),
            pltpu.VMEM((E, D), BF16),
            pltpu.VMEM((E, D), F32),
            pltpu.VMEM((E, D), BF16),
            pltpu.VMEM((E, D), BF16),
            pltpu.VMEM((E, D), BF16),
            dma((8,)),
            dma((2,)),
            dma((2,)),
            dma((2, 2, 4, 2)),
            dma((2,)),
            dma((SUB,)), dma((SUB, 4)),
            dma((SUB,)), dma((SUB, 4)),
            dma((SUB,)), dma((SUB, 4)),
            dma((3,)), dma((3,)),
        ],
        compiler_params=pltpu.CompilerParams(
            collective_id=0, has_side_effects=True, vmem_limit_bytes=60 << 20
        ),
        name="edge_layers",
    )(
        block_target[0, 0], block_source[0, 0], block_count[0], edge_states[0, 0],
        triplet_coeff[0, 0], reverse_slot[0], jnp.swapaxes(w_proj, 1, 2), w_up, w_in, w_out,
        norm_gain,
    )
    return out[None, None]


def solution(mesh):
    return jax.shard_map(
        local,
        mesh=mesh,
        in_specs=(
            P("src", "tgt", None, None),
            P("src", "tgt", None, None, None),
            P("src", "tgt", None),
            P("src", "tgt", None),
            P("src", "tgt"),
            P("src", "tgt", None),
            P(),
            P(),
            P(),
            P(),
            P(),
        ),
        out_specs=P("src", "tgt", None, None),
        check_vma=False,
    )
```

time: 396 us -> 122 us (0.31)
  the two profiles are of different devices: /device:TPU:1 before, /device:TPU:32 now
where the time goes in v1:
time: 122 us
  Pallas kernels  119 us (98%)
  local copies, waits for them, and re-layouts  2.26 us (2%)
    pallas_call x1, Pallas kernels, local(): pl.pallas_call(kernel, out_shape=jax.ShapeDtypeStruct((E, D), BF16), in_s...  119 us

profile of v1, /device:TPU:32, one launch (start us, length us, event | category | flops | bytes accessed | tf_op | source)
XLA Modules:
  0.0 122.3 jit_solution(15616920171400475308)
XLA Ops:
  0.7 119.4 %edge_layers.1 = bf16[512,1024]{1,0:T(8,128)(2,1)} custom-call(s32[16]{0:T(128)} %bitcast.14, s32[16]{0:T(128)} %bitcast.15, s32[1]{0:T(128)} %bitcast.8.cnt_s, bf16[512,1024]{1,0:T(8,128)(2,1)} %bitcast.10, bf16[16,128,128]{2,1,0:T(8,128)(2,1)} %bitcast.11, s32[1,512]{1,0:T(1,128)} %bitcast.13, bf16[2,64,1024]{2,1,0:T(8,128)(2,1)} %bitcast.12, ...), custom_call_target="tpu_custom_call" | custom-call | tf_op jit(solution)/shard_map/edge_layers/pallas_call | solution.py:450
  120.0 2.3 %copy.14 = bf16[1,1,512,1024]{3,2,1,0:T(8,128)(2,1)} copy(bf16[1,1,512,1024]{3,2,1,0:T(8,128)(2,1)} %bitcast.9) | data formatting | bytes 2097152

commit v2 on v1

--- a/solution.py
+++ b/solution.py
@@ -15,7 +15,8 @@
 T = 64
 BLK = 128
 NB = 16
-SUB = 2
+SUB = 4
+ROWS = BLK // SUB
 NBLK = 128
 
 
@@ -31,9 +32,9 @@
 
 def kernel(
     tgt_s, src_s, cnt_s, st_h, coef_h, rs_ref, wp_h, wup_h, win_h, wout_h, gain_ref, out_ref,
-    st, coef, wp, wup, win, wout, g0, g1, l1, l2, fin, perm, lhs, aggt, aggm, pbt, pbm,
+    st, coef, wp, wup, win, wout, g0, g1, l1, l2, rel, fin, perm, lhs, aggt, aggm, pbt, pbm,
     summed, branch, mst, msum, mbr, nrm, act, lsem,
-    gs, yr, zr, sr, l1s, l1r, l2s, l2r, l3s, l3r, ms, mr,
+    gs, yr, zr, sr, l1s, l1r, l2s, l2r, l2as, l2ar, l3s, l3r, ms, mr,
 ):
     k = place()
     x, y1, y0, z, c = k["x"], k["y1"], k["y0"], k["z"], k["c"]
@@ -73,8 +74,12 @@
         def _(dest=dest):
             signal(dest)
 
-    for d in (ypart, zup, zdn, sib):
-        signal(d)
+    ys = [(y1 * 2 + y0 + i) % 4 for i in range(1, 4)]
+    for yy in ys:
+        signal(device(x, yy // 2, yy % 2, z, c))
+    for i in (1, 2, 4, 6, 7):
+        signal(device(x, y1, y0, (z + i) % 8, c))
+    signal(sib)
     for xx in xs:
         signal(device(xx, y1, y0, z, c))
 
@@ -103,7 +108,7 @@
     put_own(g0, proj_t(0, st[...]))
 
     n_own2 = (y0 == z1).astype(jnp.int32)
-    pl.semaphore_wait(bar, 4 + 3 + 4 - n_own2 + not_diag.astype(jnp.int32))
+    pl.semaphore_wait(bar, 9 + 3 + 4 - n_own2 + not_diag.astype(jnp.int32))
 
     def remote(src, dst, ss, rs, d):
         return pltpu.make_async_remote_copy(
@@ -111,61 +116,65 @@
         )
 
     def make_gather(l, g):
-        def piece(col, zz, lo=0, n=4):
-            return g.at[pl.ds((col * 16 + zz * 2 + c) * 4 + lo, n)]
+        def half(col, zz, h):
+            return g.at[pl.ds((col * 16 + zz * 2 + c) * 4 + 2 * h, 2)]
+
+        def origin(direction, dist):
+            return (z + 8 - dist) % 8 if direction == 0 else (z + dist) % 8
 
         def to_sib(p):
             remote(p, p, gs.at[l], sr.at[l], sib).start()
 
-        def z_copy(p, direction, dist, b):
+        def z_copy(p, direction, dist, h):
             return remote(
-                p, p, gs.at[l], zr.at[l, direction, dist - 1, b], zup if direction == 0 else zdn
+                p, p, gs.at[l], zr.at[l, direction, dist - 1, h], zup if direction == 0 else zdn
             )
 
-        def part(direction, dist, b, at_dist):
-            col = y1 if b == 0 else 1 - y1
-            zz = (z + 8 - at_dist) % 8 if direction == 0 else (z + at_dist) % 8
-            if dist == 4:
-                return piece(col, zz, 0 if direction == 0 else 2, 2)
-            return piece(col, zz)
+        def y_copy(p, direction, dist, h):
+            i = dist if direction == 0 or dist == 0 else 4 + dist
+            return remote(p, p, gs.at[l], yr.at[l, i, h], ypart)
+
+        def ways(dist, h):
+            return (0, 1) if dist < 4 else (h,)
 
         def start():
-            own = piece(y1, z)
-            for direction in (0, 1):
-                z_copy(part(direction, 1, 0, 0), direction, 1, 0).start()
-            remote(own, own, gs.at[l], yr.at[l], ypart).start()
-            to_sib(own)
-
-        def from_y():
-            other = piece(1 - y1, z)
-            remote(other, other, gs.at[l], yr.at[l], ypart).wait_recv()
-            for direction in (0, 1):
-                z_copy(part(direction, 1, 1, 0), direction, 1, 1).start()
-            to_sib(other)
-
-        def step(dist, b):
-            for direction in (0, 1):
-                got = part(direction, dist, b, dist)
-                z_copy(got, direction, dist, b).wait_recv()
-                if dist < 4:
-                    z_copy(part(direction, dist + 1, b, dist), direction, dist + 1, b).start()
+            for h in (0, 1):
+                own = half(y1, z, h)
+                for direction in (0, 1):
+                    z_copy(own, direction, 1, h).start()
+                y_copy(own, 0, 0, h).start()
+                to_sib(own)
+
+        def z_step(dist, h):
+            for direction in ways(dist, h):
+                got = half(y1, origin(direction, dist), h)
+                z_copy(got, direction, dist, h).wait_recv()
+                if direction in ways(dist + 1, h) and dist < 4:
+                    z_copy(got, direction, dist + 1, h).start()
+                y_copy(got, direction, dist, h).start()
                 to_sib(got)
 
+        def y_step(dist, h):
+            for direction in ways(dist, h) if dist else (0,):
+                got = half(1 - y1, origin(direction, dist), h)
+                y_copy(got, direction, dist, h).wait_recv()
+                to_sib(got)
+
         def finish():
-            half = g.at[pl.ds(0, 64)]
-            remote(half, half, gs.at[l], sr.at[l], sib).wait_recv()
+            all_sib = g.at[pl.ds(0, 64)]
+            remote(all_sib, all_sib, gs.at[l], sr.at[l], sib).wait_recv()
 
         def drain():
             a = g.at[pl.ds(0, 4 * 31)]
             remote(a, a, gs.at[l], sr.at[l], sib).wait_send()
 
-        return start, from_y, step, finish, drain
+        return start, z_step, y_step, finish, drain
 
     gat0 = make_gather(0, g0)
     gat1 = make_gather(1, g1)
     gat0[0]()
 
-    rows_sub = BLK // SUB
+    rows_sub = ROWS
 
     def sub(ref, slot, j):
         return ref.at[slot, pl.ds(j * rows_sub, rows_sub)]
@@ -185,32 +194,68 @@
             remote(st_sub(xx, j), sub(l1, xx, j), l1s.at[j], l1r.at[j, i], sib).wait_recv()
         pltpu.make_async_copy(st_sub(x, j), sub(l1, x, j), l1r.at[j, 3]).wait()
 
+    relay = y0 == z1
+
     def leg2_start(j):
+        there = y1 * 2 + z2
+        if j % 2:
+            for s in range(4):
+                dest, own = leg2(s)
+
+                @pl.when(jnp.logical_not(own))
+                def _(dest=dest, s=s):
+                    remote(
+                        sub(l1, s, j), sub(l2, there, j), l2s.at[j], l2r.at[j, there], dest
+                    ).start()
+
+                @pl.when(own)
+                def _(s=s):
+                    pltpu.make_async_copy(sub(l1, s, j), sub(l2, s, j), l2r.at[j, s]).start()
+
+            return
         for s in range(4):
-            dest, own = leg2(s)
-            there = y1 * 2 + z2
-
-            @pl.when(jnp.logical_not(own))
-            def _(dest=dest, s=s):
+            s1, s0 = s // 2, s % 2
+            stays = relay & (y1 == s1)
+            slot = (y1 * 2 + y0) * 2 + s0
+
+            @pl.when(jnp.logical_not(stays))
+            def _(s=s, s1=s1, slot=slot):
                 remote(
-                    sub(l1, s, j), sub(l2, there, j), l2s.at[j], l2r.at[j, there], dest
+                    sub(l1, s, j), rel.at[j // 2, slot], l2as.at[j // 2], l2ar.at[j // 2, slot],
+                    device(x, s1, z1, z, c),
                 ).start()
 
-            @pl.when(own)
-            def _(s=s):
-                pltpu.make_async_copy(sub(l1, s, j), sub(l2, s, j), l2r.at[j, s]).start()
+            @pl.when(stays)
+            def _(s=s, slot=slot):
+                pltpu.make_async_copy(
+                    sub(l1, s, j), rel.at[j // 2, slot], l2ar.at[j // 2, slot]
+                ).start()
+
+    def leg2_relay(j):
+        @pl.when(relay)
+        def _():
+            for ysrc in range(4):
+                for s0 in range(2):
+                    slot = ysrc * 2 + s0
+                    here = rel.at[j // 2, slot]
+                    t = (ysrc // 2) * 2 + z2
+                    remote(here, here, l2as.at[j // 2], l2ar.at[j // 2, slot], sib).wait_recv()
+                    stays = (z2 == s0) & (z1 == ysrc % 2)
+
+                    @pl.when(jnp.logical_not(stays))
+                    def _(here=here, t=t, s0=s0, ysrc=ysrc):
+                        remote(
+                            here, sub(l2, t, j), l2s.at[j], l2r.at[j, t],
+                            device(x, y1, y0, s0 * 4 + (ysrc % 2) * 2 + z0, c),
+                        ).start()
+
+                    @pl.when(stays)
+                    def _(here=here, t=t):
+                        pltpu.make_async_copy(here, sub(l2, t, j), l2r.at[j, t]).start()
 
     def leg2_wait(j):
         for s in range(4):
-            dest, own = leg2(s)
-
-            @pl.when(jnp.logical_not(own))
-            def _(s=s, dest=dest):
-                remote(sub(l1, s, j), sub(l2, s, j), l2s.at[j], l2r.at[j, s], dest).wait_recv()
-
-            @pl.when(own)
-            def _(s=s):
-                pltpu.make_async_copy(sub(l1, s, j), sub(l2, s, j), l2r.at[j, s]).wait()
+            remote(sub(l1, s, j), sub(l2, s, j), l2s.at[j], l2r.at[j, s], sib).wait_recv()
 
     def fin_sub(chunk, j):
         return fin.at[pl.ds(chunk * BLK + j * rows_sub, rows_sub)]
@@ -228,19 +273,30 @@
         pltpu.make_async_copy(sub(l2, x, j), fin_sub(x, j), l3r.at[j, 3]).wait()
 
     def legs_drain():
+        rows = pl.ds(0, rows_sub)
+
+        def gone(n, sem):
+            ref = l1.at[pl.ds(0, n), rows] if n <= 4 else rel.at[0, pl.ds(0, n)]
+            remote(ref, ref, sem, l1r.at[0, 0], sib).wait_send()
+
         for j in range(SUB):
-            rows = pl.ds(0, rows_sub)
-            three, four = l1.at[pl.ds(0, 3), rows], l1.at[pl.ds(0, 4), rows]
-            remote(three, three, l1s.at[j], l1r.at[j, 0], sib).wait_send()
-            remote(three, three, l3s.at[j], l3r.at[j, 0], sib).wait_send()
-
-            @pl.when(y0 == z1)
-            def _(j=j, three=three):
-                remote(three, three, l2s.at[j], l2r.at[j, 0], sib).wait_send()
-
-            @pl.when(y0 != z1)
-            def _(j=j, four=four):
-                remote(four, four, l2s.at[j], l2r.at[j, 0], sib).wait_send()
+            gone(3, l1s.at[j])
+            gone(3, l3s.at[j])
+
+            @pl.when(relay)
+            def _(j=j):
+                if j % 2:
+                    gone(3, l2s.at[j])
+                else:
+                    gone(2, l2as.at[j // 2])
+                    gone(6, l2s.at[j])
+
+            @pl.when(jnp.logical_not(relay))
+            def _(j=j):
+                if j % 2:
+                    gone(4, l2s.at[j])
+                else:
+                    gone(4, l2as.at[j // 2])
 
     def swap_start(i, src, dst):
         @pl.when(not_diag)
@@ -280,38 +336,27 @@
     def permute_t(val):
         return jnp.dot(val, perm[...], preferred_element_type=F32)
 
-    def norm(l, rows_ref, agg, sum_ref):
+    def layer(l, rows_ref, agg, sum_ref, br):
         def body(r, _):
-            rows = pl.ds(pl.multiple_of(r * BLK, BLK), BLK)
-            up = lax.dot_general(
-                agg[:, rows], wup[l], (((0,), (0,)), ((), ())), preferred_element_type=F32
-            )
-            s = rows_ref[rows, :].astype(F32) + up
-            sum_ref[rows, :] = s
-            scale = lax.rsqrt(jnp.mean(s * s, axis=-1, keepdims=True) + 1e-06)
-            nrm[rows, :] = (gain_ref[l : l + 1, :] * s * scale).astype(BF16)
-            return 0
-
-        lax.fori_loop(0, 4, body, 0)
-
-    def hidden(l):
-        def body(n, _):
-            cols = pl.ds(pl.multiple_of(n * 256, 256), 256)
-            h = jnp.dot(nrm[...], win[l, :, cols], preferred_element_type=F32)
-            act[:, cols] = (h / (1.0 + jnp.exp(-h))).astype(BF16)
-            return 0
-
-        lax.fori_loop(0, 4, body, 0)
-
-    def outer(l, br):
-        def body(n, _):
-            cols = pl.ds(pl.multiple_of(n * 256, 256), 256)
-            br[:, cols] = jnp.dot(
-                act[...], wout[l, :, cols], preferred_element_type=F32
+            for i in range(2):
+                rows = pl.ds(pl.multiple_of(r * 256 + i * BLK, BLK), BLK)
+                up = lax.dot_general(
+                    agg[:, rows], wup[l], (((0,), (0,)), ((), ())), preferred_element_type=F32
+                )
+                s = rows_ref[rows, :].astype(F32) + up
+                sum_ref[rows, :] = s
+                scale = lax.rsqrt(jnp.mean(s * s, axis=-1, keepdims=True) + 1e-06)
+                nrm[rows, :] = (gain_ref[l : l + 1, :] * s * scale).astype(BF16)
+            rows = pl.ds(pl.multiple_of(r * 256, 256), 256)
+            h = jnp.dot(nrm[rows, :], win[l], preferred_element_type=F32)
+            h = 0.5 * h
+            act[rows, :] = (h + h * jnp.tanh(h)).astype(BF16)
+            br[rows, :] = jnp.dot(
+                act[rows, :], wout[l], preferred_element_type=F32
             ).astype(BF16)
             return 0
 
-        lax.fori_loop(0, 4, body, 0)
+        lax.fori_loop(0, 2, body, 0)
 
     def by_rows(f):
         def body(r, _):
@@ -333,30 +378,43 @@
 
     lax.fori_loop(0, 4, onehot_body, 0)
 
-    start, from_y, step, finish, drain0 = gat0
-    step(1, 0)
-    from_y()
-    step(1, 1)
-    step(2, 0)
+    start, z_step, y_step, finish, drain0 = gat0
+    z_step(1, 0)
+    z_step(1, 1)
+    y_step(0, 0)
+    y_step(0, 1)
+    z_step(2, 0)
+    z_step(2, 1)
+    y_step(1, 0)
+    y_step(1, 1)
     leg1_wait(0)
-    step(2, 1)
-    step(3, 0)
     leg2_start(0)
-    step(3, 1)
-    step(4, 0)
-    step(4, 1)
+    z_step(3, 0)
+    z_step(3, 1)
+    y_step(2, 0)
+    y_step(2, 1)
     leg1_wait(1)
     leg2_start(1)
+    z_step(4, 0)
+    z_step(4, 1)
+    y_step(3, 0)
+    y_step(3, 1)
+    leg1_wait(2)
+    leg2_start(2)
+    leg2_relay(0)
+    y_step(4, 0)
+    y_step(4, 1)
     finish()
 
     loads[2].wait()
     triplets(g0, aggt.at[0])
     swap_start(0, aggt.at[0], aggm.at[0])
+    leg1_wait(3)
+    leg2_start(3)
+    leg2_relay(2)
     for i in (3, 4, 5):
         loads[i].wait()
-    norm(0, st, aggt.at[0], summed)
-    hidden(0)
-    outer(0, branch)
+    layer(0, st, aggt.at[0], summed, branch)
     pbt[...] = proj_t(1, branch[...]).astype(BF16)
     swap_start(1, pbt, pbm)
 
@@ -365,44 +423,55 @@
 
     by_rows(part_sum)
     half1 = proj_t(1, nrm[...])
+    leg2_wait(0)
+    leg3_start(0)
+    leg2_wait(1)
+    leg3_start(1)
     swap_wait(1, pbt, pbm)
     put_own(g1, half1 + permute_t(pbm[...]))
-    start, from_y, step, finish, drain1 = gat1
+    start, z_step, y_step, finish, drain1 = gat1
     start()
-    leg2_wait(0)
-    leg3_start(0)
-    step(1, 0)
-    from_y()
-    step(1, 1)
-    step(2, 0)
-    step(2, 1)
-    step(3, 0)
-    step(3, 1)
-    step(4, 0)
-    step(4, 1)
-    leg2_wait(1)
-    leg3_start(1)
+    z_step(1, 0)
+    z_step(1, 1)
+    y_step(0, 0)
+    y_step(0, 1)
+    leg2_wait(2)
+    leg3_start(2)
+    z_step(2, 0)
+    z_step(2, 1)
+    y_step(1, 0)
+    y_step(1, 1)
+    leg2_wait(3)
+    leg3_start(3)
+    z_step(3, 0)
+    z_step(3, 1)
+    y_step(2, 0)
+    y_step(2, 1)
+    z_step(4, 0)
+    z_step(4, 1)
+    y_step(3, 0)
+    y_step(3, 1)
+    y_step(4, 0)
+    y_step(4, 1)
+
+    swap_wait(0, aggt.at[0], aggm.at[0])
+    act[0:T, 0:E] = permute_t(aggm[0]).astype(BF16)
+    aggm[0] = act[0:T, 0:E]
+    for j in range(SUB):
+        leg3_wait(j)
+
+    def take_rows(r, _):
+        rows = pl.ds(pl.multiple_of(r * 256, 256), 256)
+        mst[rows, :] = lax.dot_general(
+            perm[:, rows], fin[...], (((0,), (0,)), ((), ())), preferred_element_type=F32
+        ).astype(BF16)
+        return 0
+
+    lax.fori_loop(0, 2, take_rows, 0)
     finish()
     triplets(g1, aggt.at[1])
     swap_start(2, aggt.at[1], aggm.at[1])
-
-    swap_wait(0, aggt.at[0], aggm.at[0])
-    act[0:T, 0:E] = permute_t(aggm[0]).astype(BF16)
-    aggm[0] = act[0:T, 0:E]
-    leg3_wait(0)
-    leg3_wait(1)
-
-    def take_rows(n, _):
-        cols = pl.ds(pl.multiple_of(n * 256, 256), 256)
-        mst[:, cols] = lax.dot_general(
-            perm[...], fin[:, cols], (((0,), (0,)), ((), ())), preferred_element_type=F32
-        ).astype(BF16)
-        return 0
-
-    lax.fori_loop(0, 4, take_rows, 0)
-    norm(0, mst, aggm.at[0], msum)
-    hidden(0)
-    outer(0, mbr)
+    layer(0, mst, aggm.at[0], msum, mbr)
 
     def next_state(rows):
         b = branch[rows, :].astype(F32)
@@ -415,15 +484,11 @@
 
     for i in (6, 7):
         loads[i].wait()
-    norm(1, st, aggt.at[1], summed)
-    hidden(1)
-    outer(1, branch)
+    layer(1, st, aggt.at[1], summed, branch)
     swap_wait(2, aggt.at[1], aggm.at[1])
     act[0:T, 0:E] = permute_t(aggm[1]).astype(BF16)
     aggm[1] = act[0:T, 0:E]
-    norm(1, mst, aggm.at[1], msum)
-    hidden(1)
-    outer(1, mbr)
+    layer(1, mst, aggm.at[1], msum, mbr)
 
     def final(rows):
         out_ref[rows, :] = (
@@ -445,7 +510,7 @@
 ):
     vmem = pl.BlockSpec(memory_space=pltpu.VMEM)
     smem = pl.BlockSpec(memory_space=pltpu.SMEM)
-    hbm = pl.BlockSpec(memory_space=pl.ANY)
+    hbm = pl.BlockSpec(memory_space=pltpu.HBM)
     dma = pltpu.SemaphoreType.DMA
     out = pl.pallas_call(
         kernel,
@@ -463,6 +528,7 @@
             pltpu.VMEM((NBLK, T, BLK), BF16),
             pltpu.VMEM((4, BLK, D), BF16),
             pltpu.VMEM((4, BLK, D), BF16),
+            pltpu.VMEM((SUB // 2, 8, ROWS, D), BF16),
             pltpu.VMEM((E, D), BF16),
             pltpu.VMEM((E, E), BF16),
             pltpu.VMEM((4 * T, NB * BLK), BF16),
@@ -479,16 +545,17 @@
             pltpu.VMEM((E, D), BF16),
             dma((8,)),
             dma((2,)),
-            dma((2,)),
+            dma((2, 9, 2)),
             dma((2, 2, 4, 2)),
             dma((2,)),
             dma((SUB,)), dma((SUB, 4)),
             dma((SUB,)), dma((SUB, 4)),
+            dma((SUB // 2,)), dma((SUB // 2, 8)),
             dma((SUB,)), dma((SUB, 4)),
             dma((3,)), dma((3,)),
         ],
         compiler_params=pltpu.CompilerParams(
-            collective_id=0, has_side_effects=True, vmem_limit_bytes=60 << 20
+            collective_id=0, has_side_effects=True, vmem_limit_bytes=50 << 20
         ),
         name="edge_layers",
     )(

time: 122 us -> 98.5 us (0.81)
  the two profiles are of different devices: /device:TPU:32 before, /device:TPU:1 now
where the time goes in v2:
time: 98.5 us; the launch traced here: 98 us
  Pallas kernels  89.6 us (91%)
  local copies, waits for them, and re-layouts  7.82 us (8%)
    pallas_call x1, Pallas kernels, local(): pl.pallas_call(kernel, out_shape=jax.ShapeDtypeStruct((E, D), BF16), in_s...  89.6 us
    unnamed x17, local copies, waits for them, and re-layouts  7.82 us

profile of v2, /device:TPU:1, one launch (start us, length us, event | category | flops | bytes accessed | tf_op | source)
XLA Modules:
  0.0 98.0 jit_solution(4341618211101120401)
XLA Ops:
  0.7 0.0 copy-start
  0.7 1.2 %copy-done = bf16[1,1,512,1024]{3,2,1,0:T(8,128)(2,1)S(1)} copy-done((bf16[1,1,512,1024]{3,2,1,0:T(8,128)(2,1)S(1)}, bf16[1,1,512,1024]{3,2,1,0:T(8,128)(2,1)}, u32[]{:S(2)}) %copy-start) | copy-done | bytes 1048600
  1.9 0.0 copy-start.1
  1.9 1.0 %copy-done.1 = bf16[1,1,16,128,128]{4,3,2,1,0:T(8,128)(2,1)S(1)} copy-done((bf16[1,1,16,128,128]{4,3,2,1,0:T(8,128)(2,1)S(1)}, bf16[1,1,16,128,128]{4,3,2,1,0:T(8,128)(2,1)}, u32[]{:S(2)}) %copy-start.1) | copy-done | bytes 524312
  2.9 0.0 copy-start.2
  2.9 0.9 copy-done.2
  3.9 0.0 copy-start.3
  3.9 0.9 copy-done.3
  4.8 0.0 copy-start.4
  4.8 0.7 copy-done.4
  5.5 0.0 copy-start.5
  5.5 0.7 copy-done.5
  6.2 0.0 copy-start.6
  6.2 0.7 copy-done.6
  6.9 0.0 copy-start.7
  6.9 0.7 copy-done.7
  7.5 89.6 %edge_layers.1 = bf16[512,1024]{1,0:T(8,128)(2,1)S(1)} custom-call(s32[16]{0:T(128)S(1)} %bitcast.14, s32[16]{0:T(128)S(1)} %bitcast.15, s32[1]{0:T(128)} %bitcast.8.cnt_s, bf16[512,1024]{1,0:T(8,128)(2,1)S(1)} %bitcast.10, bf16[16,128,128]{2,1,0:T(8,128)(2,1)S(1)} %bitcast.11, s32[1,512]{1,0:T(1,128)S(1)} %bitcast.13, bf16[2,64,1024]{2,1,0:T(8,128)(2,1)S(1)} %bitcast.12, ...), custom_call_target="tpu_custom_call" | custom-call | tf_op jit(solution)/shard_map/edge_layers/pallas_call | solution.py:515
  97.1 1.0 copy.14
Async XLA Ops:
  0.7 1.2 %copy-start = (bf16[1,1,512,1024]{3,2,1,0:T(8,128)(2,1)S(1)}, bf16[1,1,512,1024]{3,2,1,0:T(8,128)(2,1)}, u32[]{:S(2)}) copy-start(bf16[1,1,512,1024]{3,2,1,0:T(8,128)(2,1)} %param.11) | copy-start | bytes 3145732
  1.9 1.0 %copy-start.1 = (bf16[1,1,16,128,128]{4,3,2,1,0:T(8,128)(2,1)S(1)}, bf16[1,1,16,128,128]{4,3,2,1,0:T(8,128)(2,1)}, u32[]{:S(2)}) copy-start(bf16[1,1,16,128,128]{4,3,2,1,0:T(8,128)(2,1)} %param.12) | copy-start | bytes 1572868
  2.9 0.9 copy-start.2
  3.9 0.9 copy-start.3
  4.8 0.7 copy-start.4
  5.5 0.7 copy-start.5
  6.2 0.7 copy-start.6
  6.9 0.7 copy-start.7

commit v3 on v2

--- a/solution.py
+++ b/solution.py
@@ -115,9 +115,16 @@
             src_ref=src, dst_ref=dst, send_sem=ss, recv_sem=rs, device_id=d, device_id_type=MESH
         )
 
+    zup2 = device(x, y1, y0, (z + 2) % 8, c)
+    zdn2 = device(x, y1, y0, (z + 6) % 8, c)
+
     def make_gather(l, g):
-        def half(col, zz, h):
-            return g.at[pl.ds((col * 16 + zz * 2 + c) * 4 + 2 * h, 2)]
+        def half(kind, zz):
+            col = 1 - y1 if kind == 2 else y1
+            return g.at[pl.ds((col * 16 + zz * 2 + c) * 4 + 2 * (kind % 2), 2)]
+
+        def other(zz):
+            return g.at[pl.ds(((1 - y1) * 16 + zz * 2 + c) * 4 + 2, 2)]
 
         def origin(direction, dist):
             return (z + 8 - dist) % 8 if direction == 0 else (z + dist) % 8
@@ -125,39 +132,52 @@
         def to_sib(p):
             remote(p, p, gs.at[l], sr.at[l], sib).start()
 
-        def z_copy(p, direction, dist, h):
-            return remote(
-                p, p, gs.at[l], zr.at[l, direction, dist - 1, h], zup if direction == 0 else zdn
-            )
+        def z_copy(p, direction, dist, kind):
+            if dist == 4:
+                d = zup2 if direction == 0 else zdn2
+            else:
+                d = zup if direction == 0 else zdn
+            return remote(p, p, gs.at[l], zr.at[l, direction, dist - 1, kind], d)
 
         def y_copy(p, direction, dist, h):
             i = dist if direction == 0 or dist == 0 else 4 + dist
             return remote(p, p, gs.at[l], yr.at[l, i, h], ypart)
 
-        def ways(dist, h):
-            return (0, 1) if dist < 4 else (h,)
+        def ways(dist, kind):
+            return (0, 1) if dist < 4 else ((0,) if kind == 0 else (1,))
 
         def start():
-            for h in (0, 1):
-                own = half(y1, z, h)
+            for kind in (0, 1):
+                own = half(kind, z)
                 for direction in (0, 1):
-                    z_copy(own, direction, 1, h).start()
-                y_copy(own, 0, 0, h).start()
+                    z_copy(own, direction, 1, kind).start()
+                y_copy(own, 0, 0, kind).start()
                 to_sib(own)
 
-        def z_step(dist, h):
-            for direction in ways(dist, h):
-                got = half(y1, origin(direction, dist), h)
-                z_copy(got, direction, dist, h).wait_recv()
-                if direction in ways(dist + 1, h) and dist < 4:
-                    z_copy(got, direction, dist + 1, h).start()
-                y_copy(got, direction, dist, h).start()
-                to_sib(got)
-
-        def y_step(dist, h):
-            for direction in ways(dist, h) if dist else (0,):
-                got = half(1 - y1, origin(direction, dist), h)
-                y_copy(got, direction, dist, h).wait_recv()
+        def z_step(dist, kinds=(0, 1, 2)):
+            for kind in kinds:
+                for direction in ways(dist, kind):
+                    got = half(kind, origin(direction, dist))
+                    z_copy(got, direction, dist, kind).wait_recv()
+                    if dist < 3:
+                        z_copy(got, direction, dist + 1, kind).start()
+                    if dist == 2 and direction in ways(4, kind):
+                        z_copy(got, direction, 4, kind).start()
+                    if kind == 1:
+                        y_copy(got, direction, dist, 1).start()
+                    to_sib(got)
+
+        def y_first():
+            got = half(2, z)
+            y_copy(got, 0, 0, 0).wait_recv()
+            for direction in (0, 1):
+                z_copy(got, direction, 1, 2).start()
+            to_sib(got)
+
+        def y_step(dist):
+            for direction in ways(dist, 1) if dist else (0,):
+                got = other(origin(direction, dist))
+                y_copy(got, direction, dist, 1).wait_recv()
                 to_sib(got)
 
         def finish():
@@ -168,7 +188,7 @@
             a = g.at[pl.ds(0, 4 * 31)]
             remote(a, a, gs.at[l], sr.at[l], sib).wait_send()
 
-        return start, z_step, y_step, finish, drain
+        return start, z_step, y_first, y_step, finish, drain
 
     gat0 = make_gather(0, g0)
     gat1 = make_gather(1, g1)
@@ -187,49 +207,48 @@
             remote(
                 st_sub(xx, j), sub(l1, x, j), l1s.at[j], l1r.at[j, 3 - 1 - i], device(xx, y1, y0, z, c)
             ).start()
-        pltpu.make_async_copy(st_sub(x, j), sub(l1, x, j), l1r.at[j, 3]).start()
 
     def leg1_wait(j):
         for i, xx in enumerate(xs):
             remote(st_sub(xx, j), sub(l1, xx, j), l1s.at[j], l1r.at[j, i], sib).wait_recv()
-        pltpu.make_async_copy(st_sub(x, j), sub(l1, x, j), l1r.at[j, 3]).wait()
 
     relay = y0 == z1
 
+    def leg2_one(j, s, src):
+        there = y1 * 2 + z2
+        s1, s0 = s // 2, s % 2
+        if j % 2:
+            dest, own = leg2(s)
+
+            @pl.when(jnp.logical_not(own))
+            def _():
+                remote(src, sub(l2, there, j), l2s.at[j], l2r.at[j, there], dest).start()
+
+            @pl.when(own)
+            def _():
+                pltpu.make_async_copy(src, sub(l2, s, j), l2r.at[j, s]).start()
+
+            return
+        stays = relay & (y1 == s1)
+        slot = (y1 * 2 + y0) * 2 + s0
+
+        @pl.when(jnp.logical_not(stays))
+        def _():
+            remote(
+                src, rel.at[j // 2, slot], l2as.at[j // 2], l2ar.at[j // 2, slot],
+                device(x, s1, z1, z, c),
+            ).start()
+
+        @pl.when(stays)
+        def _():
+            pltpu.make_async_copy(src, rel.at[j // 2, slot], l2ar.at[j // 2, slot]).start()
+
+    def leg2_own(j):
+        leg2_one(j, x, st_sub(x, j))
+
     def leg2_start(j):
-        there = y1 * 2 + z2
-        if j % 2:
-            for s in range(4):
-                dest, own = leg2(s)
-
-                @pl.when(jnp.logical_not(own))
-                def _(dest=dest, s=s):
-                    remote(
-                        sub(l1, s, j), sub(l2, there, j), l2s.at[j], l2r.at[j, there], dest
-                    ).start()
-
-                @pl.when(own)
-                def _(s=s):
-                    pltpu.make_async_copy(sub(l1, s, j), sub(l2, s, j), l2r.at[j, s]).start()
-
-            return
-        for s in range(4):
-            s1, s0 = s // 2, s % 2
-            stays = relay & (y1 == s1)
-            slot = (y1 * 2 + y0) * 2 + s0
-
-            @pl.when(jnp.logical_not(stays))
-            def _(s=s, s1=s1, slot=slot):
-                remote(
-                    sub(l1, s, j), rel.at[j // 2, slot], l2as.at[j // 2], l2ar.at[j // 2, slot],
-                    device(x, s1, z1, z, c),
-                ).start()
-
-            @pl.when(stays)
-            def _(s=s, slot=slot):
-                pltpu.make_async_copy(
-                    sub(l1, s, j), rel.at[j // 2, slot], l2ar.at[j // 2, slot]
-                ).start()
+        for xx in xs:
+            leg2_one(j, xx, sub(l1, xx, j))
 
     def leg2_relay(j):
         @pl.when(relay)
@@ -336,24 +355,29 @@
     def permute_t(val):
         return jnp.dot(val, perm[...], preferred_element_type=F32)
 
+    def layer_half(l, rows_ref, agg, sum_ref, br, r):
+        def norm(i, _):
+            rows = pl.ds(pl.multiple_of(r * 256 + i * BLK, BLK), BLK)
+            up = lax.dot_general(
+                agg[:, rows], wup[l], (((0,), (0,)), ((), ())), preferred_element_type=F32
+            )
+            s = rows_ref[rows, :].astype(F32) + up
+            sum_ref[rows, :] = s
+            scale = lax.rsqrt(jnp.mean(s * s, axis=-1, keepdims=True) + 1e-06)
+            nrm[rows, :] = (gain_ref[l : l + 1, :] * s * scale).astype(BF16)
+            return 0
+
+        for i in range(2):
+            norm(i, 0)
+        rows = pl.ds(r * 256 if isinstance(r, int) else pl.multiple_of(r * 256, 256), 256)
+        h = jnp.dot(nrm[rows, :], win[l], preferred_element_type=F32)
+        h = 0.5 * h
+        act[rows, :] = (h + h * jnp.tanh(h)).astype(BF16)
+        br[rows, :] = jnp.dot(act[rows, :], wout[l], preferred_element_type=F32).astype(BF16)
+
     def layer(l, rows_ref, agg, sum_ref, br):
         def body(r, _):
-            for i in range(2):
-                rows = pl.ds(pl.multiple_of(r * 256 + i * BLK, BLK), BLK)
-                up = lax.dot_general(
-                    agg[:, rows], wup[l], (((0,), (0,)), ((), ())), preferred_element_type=F32
-                )
-                s = rows_ref[rows, :].astype(F32) + up
-                sum_ref[rows, :] = s
-                scale = lax.rsqrt(jnp.mean(s * s, axis=-1, keepdims=True) + 1e-06)
-                nrm[rows, :] = (gain_ref[l : l + 1, :] * s * scale).astype(BF16)
-            rows = pl.ds(pl.multiple_of(r * 256, 256), 256)
-            h = jnp.dot(nrm[rows, :], win[l], preferred_element_type=F32)
-            h = 0.5 * h
-            act[rows, :] = (h + h * jnp.tanh(h)).astype(BF16)
-            br[rows, :] = jnp.dot(
-                act[rows, :], wout[l], preferred_element_type=F32
-            ).astype(BF16)
+            layer_half(l, rows_ref, agg, sum_ref, br, r)
             return 0
 
         lax.fori_loop(0, 2, body, 0)
@@ -378,81 +402,74 @@
 
     lax.fori_loop(0, 4, onehot_body, 0)
 
-    start, z_step, y_step, finish, drain0 = gat0
-    z_step(1, 0)
-    z_step(1, 1)
-    y_step(0, 0)
-    y_step(0, 1)
-    z_step(2, 0)
-    z_step(2, 1)
-    y_step(1, 0)
-    y_step(1, 1)
+    _, z_step, y_first, y_step, finish, drain0 = gat0
+    z_step(1, (0, 1))
+    leg2_own(0)
+    leg2_own(1)
+    y_first()
+    y_step(0)
+    z_step(2, (0, 1))
+    z_step(1, (2,))
     leg1_wait(0)
     leg2_start(0)
-    z_step(3, 0)
-    z_step(3, 1)
-    y_step(2, 0)
-    y_step(2, 1)
+    z_step(2, (2,))
+    y_step(1)
+    leg2_own(2)
+    leg2_own(3)
     leg1_wait(1)
     leg2_start(1)
-    z_step(4, 0)
-    z_step(4, 1)
-    y_step(3, 0)
-    y_step(3, 1)
+    z_step(3)
+    y_step(2)
     leg1_wait(2)
     leg2_start(2)
     leg2_relay(0)
-    y_step(4, 0)
-    y_step(4, 1)
+    z_step(4)
+    y_step(3)
+    leg1_wait(3)
+    leg2_start(3)
+    y_step(4)
     finish()
 
     loads[2].wait()
     triplets(g0, aggt.at[0])
     swap_start(0, aggt.at[0], aggm.at[0])
-    leg1_wait(3)
-    leg2_start(3)
     leg2_relay(2)
     for i in (3, 4, 5):
         loads[i].wait()
-    layer(0, st, aggt.at[0], summed, branch)
+    layer_half(0, st, aggt.at[0], summed, branch, 0)
+    leg2_wait(0)
+    leg3_start(0)
+    layer_half(0, st, aggt.at[0], summed, branch, 1)
     pbt[...] = proj_t(1, branch[...]).astype(BF16)
     swap_start(1, pbt, pbm)
+    leg2_wait(1)
+    leg3_start(1)
 
     def part_sum(rows):
         nrm[rows, :] = (summed[rows, :] + branch[rows, :].astype(F32)).astype(BF16)
 
     by_rows(part_sum)
     half1 = proj_t(1, nrm[...])
-    leg2_wait(0)
-    leg3_start(0)
-    leg2_wait(1)
-    leg3_start(1)
+    leg2_wait(2)
+    leg3_start(2)
     swap_wait(1, pbt, pbm)
     put_own(g1, half1 + permute_t(pbm[...]))
-    start, z_step, y_step, finish, drain1 = gat1
+    start, z_step, y_first, y_step, finish, drain1 = gat1
     start()
-    z_step(1, 0)
-    z_step(1, 1)
-    y_step(0, 0)
-    y_step(0, 1)
-    leg2_wait(2)
-    leg3_start(2)
-    z_step(2, 0)
-    z_step(2, 1)
-    y_step(1, 0)
-    y_step(1, 1)
+    z_step(1, (0, 1))
+    y_first()
+    y_step(0)
+    z_step(2, (0, 1))
+    z_step(1, (2,))
     leg2_wait(3)
     leg3_start(3)
-    z_step(3, 0)
-    z_step(3, 1)
-    y_step(2, 0)
-    y_step(2, 1)
-    z_step(4, 0)
-    z_step(4, 1)
-    y_step(3, 0)
-    y_step(3, 1)
-    y_step(4, 0)
-    y_step(4, 1)
+    z_step(2, (2,))
+    y_step(1)
+    z_step(3)
+    y_step(2)
+    z_step(4)
+    y_step(3)
+    y_step(4)
 
     swap_wait(0, aggt.at[0], aggm.at[0])
     act[0:T, 0:E] = permute_t(aggm[0]).astype(BF16)
@@ -546,7 +563,7 @@
             dma((8,)),
             dma((2,)),
             dma((2, 9, 2)),
-            dma((2, 2, 4, 2)),
+            dma((2, 2, 4, 3)),
             dma((2,)),
             dma((SUB,)), dma((SUB, 4)),
             dma((SUB,)), dma((SUB, 4)),
@@ -555,7 +572,7 @@
             dma((3,)), dma((3,)),
         ],
         compiler_params=pltpu.CompilerParams(
-            collective_id=0, has_side_effects=True, vmem_limit_bytes=50 << 20
+            collective_id=0, has_side_effects=True, vmem_limit_bytes=56 << 20
         ),
         name="edge_layers",
     )(

time: 98.5 us -> 97.1 us (0.986)
  local copies, waits for them, and re-layouts: 7.82 us -> 2.26 us
  Pallas kernels: 89.6 us -> 94 us
    unnamed x17 -> x1, local copies, waits for them, and re-layouts: 7.82 us -> 2.26 us
    pallas_call x1, Pallas kernels: 89.6 us -> 94 us  [local(): pl.pallas_call(kernel, out_shape=jax.ShapeDtypeStruct((E, D), BF16), in_s...]
where the time goes in v3:
time: 97.1 us; the launch traced here: 97 us
  Pallas kernels  94 us (97%)
  local copies, waits for them, and re-layouts  2.26 us (2%)
    pallas_call x1, Pallas kernels, local(): pl.pallas_call(kernel, out_shape=jax.ShapeDtypeStruct((E, D), BF16), in_s...  94 us
    unnamed x1, local copies, waits for them, and re-layouts  2.26 us

profile of v3, /device:TPU:1, one launch (start us, length us, event | category | flops | bytes accessed | tf_op | source)
XLA Modules:
  0.0 97.0 jit_solution(14495414017368218562)
XLA Ops:
  0.7 94.0 %edge_layers.1 = bf16[512,1024]{1,0:T(8,128)(2,1)} custom-call(s32[16]{0:T(128)} %bitcast.14, s32[16]{0:T(128)} %bitcast.15, s32[1]{0:T(128)} %bitcast.8.cnt_s, bf16[512,1024]{1,0:T(8,128)(2,1)} %bitcast.10, bf16[16,128,128]{2,1,0:T(8,128)(2,1)} %bitcast.11, s32[1,512]{1,0:T(1,128)} %bitcast.13, bf16[2,64,1024]{2,1,0:T(8,128)(2,1)} %bitcast.12, ...), custom_call_target="tpu_custom_call" | custom-call | tf_op jit(solution)/shard_map/edge_layers/pallas_call | solution.py:532
  94.7 2.3 %copy.14 = bf16[1,1,512,1024]{3,2,1,0:T(8,128)(2,1)} copy(bf16[1,1,512,1024]{3,2,1,0:T(8,128)(2,1)} %bitcast.9) | data formatting | bytes 2097152

commit v4 on v3

--- a/solution.py
+++ b/solution.py
@@ -77,9 +77,16 @@
     ys = [(y1 * 2 + y0 + i) % 4 for i in range(1, 4)]
     for yy in ys:
         signal(device(x, yy // 2, yy % 2, z, c))
-    for i in (1, 2, 4, 6, 7):
+    for i in (1, 2, 6, 7):
         signal(device(x, y1, y0, (z + i) % 8, c))
     signal(sib)
+    z_rel = x0 * 4 + y0 * 2 + z0
+    for kk in range(4):
+
+        @pl.when(jnp.logical_not((kk == x) & (z_rel == z)))
+        def _(kk=kk):
+            signal(device(kk, y1, y0, z_rel, c))
+
     for xx in xs:
         signal(device(xx, y1, y0, z, c))
 
@@ -108,7 +115,8 @@
     put_own(g0, proj_t(0, st[...]))
 
     n_own2 = (y0 == z1).astype(jnp.int32)
-    pl.semaphore_wait(bar, 9 + 3 + 4 - n_own2 + not_diag.astype(jnp.int32))
+    n_final = n_own2 * (8 - (x0 == z2).astype(jnp.int32))
+    pl.semaphore_wait(bar, 8 + 3 + 4 - n_own2 + not_diag.astype(jnp.int32) + n_final)
 
     def remote(src, dst, ss, rs, d):
         return pltpu.make_async_remote_copy(
@@ -119,12 +127,8 @@
     zdn2 = device(x, y1, y0, (z + 6) % 8, c)
 
     def make_gather(l, g):
-        def half(kind, zz):
-            col = 1 - y1 if kind == 2 else y1
-            return g.at[pl.ds((col * 16 + zz * 2 + c) * 4 + 2 * (kind % 2), 2)]
-
-        def other(zz):
-            return g.at[pl.ds(((1 - y1) * 16 + zz * 2 + c) * 4 + 2, 2)]
+        def half(col, zz, h):
+            return g.at[pl.ds((col * 16 + zz * 2 + c) * 4 + 2 * h, 2)]
 
         def origin(direction, dist):
             return (z + 8 - dist) % 8 if direction == 0 else (z + dist) % 8
@@ -132,53 +136,46 @@
         def to_sib(p):
             remote(p, p, gs.at[l], sr.at[l], sib).start()
 
-        def z_copy(p, direction, dist, kind):
+        def z_copy(p, direction, dist, h):
             if dist == 4:
                 d = zup2 if direction == 0 else zdn2
             else:
                 d = zup if direction == 0 else zdn
-            return remote(p, p, gs.at[l], zr.at[l, direction, dist - 1, kind], d)
+            return remote(p, p, gs.at[l], zr.at[l, direction, dist - 1, h], d)
 
         def y_copy(p, direction, dist, h):
             i = dist if direction == 0 or dist == 0 else 4 + dist
             return remote(p, p, gs.at[l], yr.at[l, i, h], ypart)
 
-        def ways(dist, kind):
-            return (0, 1) if dist < 4 else ((0,) if kind == 0 else (1,))
+        def ways(dist, h):
+            return (0, 1) if dist < 4 else (h,)
 
         def start():
-            for kind in (0, 1):
-                own = half(kind, z)
+            for h in (0, 1):
+                own = half(y1, z, h)
                 for direction in (0, 1):
-                    z_copy(own, direction, 1, kind).start()
-                y_copy(own, 0, 0, kind).start()
+                    z_copy(own, direction, 1, h).start()
+                y_copy(own, 0, 0, h).start()
                 to_sib(own)
 
-        def z_step(dist, kinds=(0, 1, 2)):
-            for kind in kinds:
-                for direction in ways(dist, kind):
-                    got = half(kind, origin(direction, dist))
-                    z_copy(got, direction, dist, kind).wait_recv()
+        def z_step(dist):
+            for h in (0, 1):
+                for direction in ways(dist, h):
+                    got = half(y1, origin(direction, dist), h)
+                    z_copy(got, direction, dist, h).wait_recv()
                     if dist < 3:
-                        z_copy(got, direction, dist + 1, kind).start()
-                    if dist == 2 and direction in ways(4, kind):
-                        z_copy(got, direction, 4, kind).start()
-                    if kind == 1:
-                        y_copy(got, direction, dist, 1).start()
+                        z_copy(got, direction, dist + 1, h).start()
+                    if dist == 2 and direction == h:
+                        z_copy(got, direction, 4, h).start()
+                    y_copy(got, direction, dist, h).start()
                     to_sib(got)
 
-        def y_first():
-            got = half(2, z)
-            y_copy(got, 0, 0, 0).wait_recv()
-            for direction in (0, 1):
-                z_copy(got, direction, 1, 2).start()
-            to_sib(got)
-
         def y_step(dist):
-            for direction in ways(dist, 1) if dist else (0,):
-                got = other(origin(direction, dist))
-                y_copy(got, direction, dist, 1).wait_recv()
-                to_sib(got)
+            for h in (0, 1):
+                for direction in ways(dist, h) if dist else (0,):
+                    got = half(1 - y1, origin(direction, dist), h)
+                    y_copy(got, direction, dist, h).wait_recv()
+                    to_sib(got)
 
         def finish():
             all_sib = g.at[pl.ds(0, 64)]
@@ -188,7 +185,7 @@
             a = g.at[pl.ds(0, 4 * 31)]
             remote(a, a, gs.at[l], sr.at[l], sib).wait_send()
 
-        return start, z_step, y_first, y_step, finish, drain
+        return start, z_step, y_step, finish, drain
 
     gat0 = make_gather(0, g0)
     gat1 = make_gather(1, g1)
@@ -201,6 +198,9 @@
 
     def st_sub(chunk, j):
         return st.at[pl.ds(chunk * BLK + j * rows_sub, rows_sub)]
+
+    def fin_sub(chunk, j):
+        return fin.at[pl.ds(chunk * BLK + j * rows_sub, rows_sub)]
 
     def leg1_start(j):
         for i, xx in enumerate(xs):
@@ -259,37 +259,33 @@
                     here = rel.at[j // 2, slot]
                     t = (ysrc // 2) * 2 + z2
                     remote(here, here, l2as.at[j // 2], l2ar.at[j // 2, slot], sib).wait_recv()
-                    stays = (z2 == s0) & (z1 == ysrc % 2)
+                    stays = (z2 == s0) & (z1 == ysrc % 2) & (t == x)
 
                     @pl.when(jnp.logical_not(stays))
                     def _(here=here, t=t, s0=s0, ysrc=ysrc):
                         remote(
-                            here, sub(l2, t, j), l2s.at[j], l2r.at[j, t],
-                            device(x, y1, y0, s0 * 4 + (ysrc % 2) * 2 + z0, c),
+                            here, fin_sub(x, j), l2s.at[j], l3r.at[j, x],
+                            device(t, y1, y0, s0 * 4 + (ysrc % 2) * 2 + z0, c),
                         ).start()
 
                     @pl.when(stays)
-                    def _(here=here, t=t):
-                        pltpu.make_async_copy(here, sub(l2, t, j), l2r.at[j, t]).start()
+                    def _(here=here):
+                        pltpu.make_async_copy(here, fin_sub(x, j), l3r.at[j, x]).start()
 
     def leg2_wait(j):
         for s in range(4):
             remote(sub(l1, s, j), sub(l2, s, j), l2s.at[j], l2r.at[j, s], sib).wait_recv()
 
-    def fin_sub(chunk, j):
-        return fin.at[pl.ds(chunk * BLK + j * rows_sub, rows_sub)]
-
     def leg3_start(j):
         for i, xx in enumerate(xs):
             remote(
-                sub(l2, xx, j), fin_sub(x, j), l3s.at[j], l3r.at[j, 3 - 1 - i], device(xx, y1, y0, z, c)
+                sub(l2, xx, j), fin_sub(x, j), l3s.at[j], l3r.at[j, x], device(xx, y1, y0, z, c)
             ).start()
-        pltpu.make_async_copy(sub(l2, x, j), fin_sub(x, j), l3r.at[j, 3]).start()
+        pltpu.make_async_copy(sub(l2, x, j), fin_sub(x, j), l3r.at[j, x]).start()
 
     def leg3_wait(j):
-        for i, xx in enumerate(xs):
-            remote(sub(l2, xx, j), fin_sub(xx, j), l3s.at[j], l3r.at[j, i], sib).wait_recv()
-        pltpu.make_async_copy(sub(l2, x, j), fin_sub(x, j), l3r.at[j, 3]).wait()
+        for k in range(4):
+            remote(sub(l2, k, j), fin_sub(k, j), l3s.at[j], l3r.at[j, k], sib).wait_recv()
 
     def legs_drain():
         rows = pl.ds(0, rows_sub)
@@ -300,7 +296,8 @@
 
         for j in range(SUB):
             gone(3, l1s.at[j])
-            gone(3, l3s.at[j])
+            if j % 2:
+                gone(3, l3s.at[j])
 
             @pl.when(relay)
             def _(j=j):
@@ -308,7 +305,14 @@
                     gone(3, l2s.at[j])
                 else:
                     gone(2, l2as.at[j // 2])
-                    gone(6, l2s.at[j])
+
+                    @pl.when(x0 == z2)
+                    def _():
+                        gone(7, l2s.at[j])
+
+                    @pl.when(x0 != z2)
+                    def _():
+                        gone(8, l2s.at[j])
 
             @pl.when(jnp.logical_not(relay))
             def _(j=j):
@@ -402,28 +406,25 @@
 
     lax.fori_loop(0, 4, onehot_body, 0)
 
-    _, z_step, y_first, y_step, finish, drain0 = gat0
-    z_step(1, (0, 1))
+    _, z_step, y_step, finish, drain0 = gat0
+    z_step(1)
     leg2_own(0)
     leg2_own(1)
-    y_first()
     y_step(0)
-    z_step(2, (0, 1))
-    z_step(1, (2,))
     leg1_wait(0)
     leg2_start(0)
-    z_step(2, (2,))
+    z_step(2)
     y_step(1)
     leg2_own(2)
     leg2_own(3)
     leg1_wait(1)
     leg2_start(1)
     z_step(3)
+    z_step(4)
     y_step(2)
     leg1_wait(2)
     leg2_start(2)
     leg2_relay(0)
-    z_step(4)
     y_step(3)
     leg1_wait(3)
     leg2_start(3)
@@ -436,44 +437,41 @@
     leg2_relay(2)
     for i in (3, 4, 5):
         loads[i].wait()
-    layer_half(0, st, aggt.at[0], summed, branch, 0)
-    leg2_wait(0)
-    leg3_start(0)
-    layer_half(0, st, aggt.at[0], summed, branch, 1)
-    pbt[...] = proj_t(1, branch[...]).astype(BF16)
-    swap_start(1, pbt, pbm)
-    leg2_wait(1)
-    leg3_start(1)
+    for r in (0, 1):
+        rows = pl.ds(r * 256, 256)
+        layer_half(0, st, aggt.at[0], summed, branch, r)
+        pbt[r] = proj_t(1, branch[rows, :]).astype(BF16)
+        swap_start(1 + r, pbt.at[r], pbm.at[r])
+        if r == 0:
+            leg2_wait(1)
+            leg3_start(1)
 
     def part_sum(rows):
         nrm[rows, :] = (summed[rows, :] + branch[rows, :].astype(F32)).astype(BF16)
 
     by_rows(part_sum)
     half1 = proj_t(1, nrm[...])
-    leg2_wait(2)
-    leg3_start(2)
-    swap_wait(1, pbt, pbm)
-    put_own(g1, half1 + permute_t(pbm[...]))
-    start, z_step, y_first, y_step, finish, drain1 = gat1
-    start()
-    z_step(1, (0, 1))
-    y_first()
-    y_step(0)
-    z_step(2, (0, 1))
-    z_step(1, (2,))
     leg2_wait(3)
     leg3_start(3)
-    z_step(2, (2,))
+    swap_wait(1, pbt.at[0], pbm.at[0])
+    swap_wait(2, pbt.at[1], pbm.at[1])
+    mirrored_pb = jnp.dot(pbm[0], perm[0:256, :], preferred_element_type=F32) + jnp.dot(
+        pbm[1], perm[256:512, :], preferred_element_type=F32
+    )
+    put_own(g1, half1 + mirrored_pb)
+    start, z_step, y_step, finish, drain1 = gat1
+    start()
+    z_step(1)
+    y_step(0)
+    z_step(2)
     y_step(1)
-    z_step(3)
-    y_step(2)
-    z_step(4)
-    y_step(3)
-    y_step(4)
-
     swap_wait(0, aggt.at[0], aggm.at[0])
     act[0:T, 0:E] = permute_t(aggm[0]).astype(BF16)
     aggm[0] = act[0:T, 0:E]
+    z_step(3)
+    z_step(4)
+    y_step(2)
+
     for j in range(SUB):
         leg3_wait(j)
 
@@ -485,10 +483,13 @@
         return 0
 
     lax.fori_loop(0, 2, take_rows, 0)
+    layer_half(0, mst, aggm.at[0], msum, mbr, 0)
+    y_step(3)
+    y_step(4)
     finish()
     triplets(g1, aggt.at[1])
-    swap_start(2, aggt.at[1], aggm.at[1])
-    layer(0, mst, aggm.at[0], msum, mbr)
+    swap_start(3, aggt.at[1], aggm.at[1])
+    layer_half(0, mst, aggm.at[0], msum, mbr, 1)
 
     def next_state(rows):
         b = branch[rows, :].astype(F32)
@@ -502,7 +503,7 @@
     for i in (6, 7):
         loads[i].wait()
     layer(1, st, aggt.at[1], summed, branch)
-    swap_wait(2, aggt.at[1], aggm.at[1])
+    swap_wait(3, aggt.at[1], aggm.at[1])
     act[0:T, 0:E] = permute_t(aggm[1]).astype(BF16)
     aggm[1] = act[0:T, 0:E]
     layer(1, mst, aggm.at[1], msum, mbr)
@@ -517,8 +518,9 @@
     drain0()
     drain1()
     swap_drain(0, aggt.at[0], aggm.at[0])
-    swap_drain(1, pbt, pbm)
-    swap_drain(2, aggt.at[1], aggm.at[1])
+    swap_drain(1, pbt.at[0], pbm.at[0])
+    swap_drain(2, pbt.at[1], pbm.at[1])
+    swap_drain(3, aggt.at[1], aggm.at[1])
 
 
 def local(
@@ -551,8 +553,8 @@
             pltpu.VMEM((4 * T, NB * BLK), BF16),
             pltpu.VMEM((2, T, E), BF16),
             pltpu.VMEM((2, T, E), BF16),
-            pltpu.VMEM((T, E), BF16),
-            pltpu.VMEM((T, E), BF16),
+            pltpu.VMEM((2, T, 256), BF16),
+            pltpu.VMEM((2, T, 256), BF16),
             pltpu.VMEM((E, D), F32),
             pltpu.VMEM((E, D), BF16),
             pltpu.VMEM((E, D), BF16),
@@ -563,13 +565,13 @@
             dma((8,)),
             dma((2,)),
             dma((2, 9, 2)),
-            dma((2, 2, 4, 3)),
+            dma((2, 2, 4, 2)),
             dma((2,)),
             dma((SUB,)), dma((SUB, 4)),
             dma((SUB,)), dma((SUB, 4)),
             dma((SUB // 2,)), dma((SUB // 2, 8)),
             dma((SUB,)), dma((SUB, 4)),
-            dma((3,)), dma((3,)),
+            dma((4,)), dma((4,)),
         ],
         compiler_params=pltpu.CompilerParams(
             collective_id=0, has_side_effects=True, vmem_limit_bytes=56 << 20

time: 97.1 us -> 91.4 us (0.941)
  Pallas kernels: 94 us -> 88.3 us
    pallas_call x1, Pallas kernels: 94 us -> 88.3 us  [local(): pl.pallas_call(kernel, out_shape=jax.ShapeDtypeStruct((E, D), BF16), in_s...]
where the time goes in v4:
time: 91.4 us; the launch traced here: 91.2 us
  Pallas kernels  88.3 us (97%)
  local copies, waits for them, and re-layouts  2.26 us (2%)
    pallas_call x1, Pallas kernels, local(): pl.pallas_call(kernel, out_shape=jax.ShapeDtypeStruct((E, D), BF16), in_s...  88.3 us
    unnamed x1, local copies, waits for them, and re-layouts  2.26 us

profile of v4, /device:TPU:1, one launch (start us, length us, event | category | flops | bytes accessed | tf_op | source)
XLA Modules:
  0.0 91.2 jit_solution(9460605971734043238)
XLA Ops:
  0.7 88.3 %edge_layers.1 = bf16[512,1024]{1,0:T(8,128)(2,1)} custom-call(s32[16]{0:T(128)} %bitcast.14, s32[16]{0:T(128)} %bitcast.15, s32[1]{0:T(128)} %bitcast.8.cnt_s, bf16[512,1024]{1,0:T(8,128)(2,1)} %bitcast.10, bf16[16,128,128]{2,1,0:T(8,128)(2,1)} %bitcast.11, s32[1,512]{1,0:T(1,128)} %bitcast.13, bf16[2,64,1024]{2,1,0:T(8,128)(2,1)} %bitcast.12, ...), custom_call_target="tpu_custom_call" | custom-call | tf_op jit(solution)/shard_map/edge_layers/pallas_call | solution.py:534
  89.0 2.3 %copy.14 = bf16[1,1,512,1024]{3,2,1,0:T(8,128)(2,1)} copy(bf16[1,1,512,1024]{3,2,1,0:T(8,128)(2,1)} %bitcast.9) | data formatting | bytes 2097152

commit v5 on v4

--- a/solution.py
+++ b/solution.py
@@ -15,7 +15,7 @@
 T = 64
 BLK = 128
 NB = 16
-SUB = 4
+SUB = 8
 ROWS = BLK // SUB
 NBLK = 128
 
@@ -31,7 +31,8 @@
 
 
 def kernel(
-    tgt_s, src_s, cnt_s, st_h, coef_h, rs_ref, wp_h, wup_h, win_h, wout_h, gain_ref, out_ref,
+    tgt_h, src_h, cnt_s, rs_h, gain_h, st_h, coef_h, wp_h, wup_h, win_h, wout_h, out_ref,
+    tgt_s, src_s, rs_ref, gain_ref,
     st, coef, wp, wup, win, wout, g0, g1, l1, l2, rel, fin, perm, lhs, aggt, aggm, pbt, pbm,
     summed, branch, mst, msum, mbr, nrm, act, lsem,
     gs, yr, zr, sr, l1s, l1r, l2s, l2r, l2as, l2ar, l3s, l3r, ms, mr,
@@ -94,7 +95,8 @@
         pltpu.make_async_copy(a, b, lsem.at[i])
         for i, (a, b) in enumerate(
             [(st_h, st), (wp_h, wp), (coef_h, coef), (wup_h, wup), (win_h.at[0], win.at[0]),
-             (wout_h.at[0], wout.at[0]), (win_h.at[1], win.at[1]), (wout_h.at[1], wout.at[1])]
+             (wout_h.at[0], wout.at[0]), (win_h.at[1], win.at[1]), (wout_h.at[1], wout.at[1]),
+             (rs_h, rs_ref), (gain_h, gain_ref), (tgt_h, tgt_s), (src_h, src_s)]
         )
     ]
     for cp in loads:
@@ -366,7 +368,8 @@
                 agg[:, rows], wup[l], (((0,), (0,)), ((), ())), preferred_element_type=F32
             )
             s = rows_ref[rows, :].astype(F32) + up
-            sum_ref[rows, :] = s
+            if sum_ref is not None:
+                sum_ref[rows, :] = s
             scale = lax.rsqrt(jnp.mean(s * s, axis=-1, keepdims=True) + 1e-06)
             nrm[rows, :] = (gain_ref[l : l + 1, :] * s * scale).astype(BF16)
             return 0
@@ -377,14 +380,17 @@
         h = jnp.dot(nrm[rows, :], win[l], preferred_element_type=F32)
         h = 0.5 * h
         act[rows, :] = (h + h * jnp.tanh(h)).astype(BF16)
-        br[rows, :] = jnp.dot(act[rows, :], wout[l], preferred_element_type=F32).astype(BF16)
+        val = jnp.dot(act[rows, :], wout[l], preferred_element_type=F32).astype(BF16)
+        if br is None:
+            out_ref[rows, :] = (
+                (summed[rows, :] + branch[rows, :].astype(F32)) + val.astype(F32)
+            ).astype(BF16)
+        else:
+            br[rows, :] = val
 
     def layer(l, rows_ref, agg, sum_ref, br):
-        def body(r, _):
+        for r in (0, 1):
             layer_half(l, rows_ref, agg, sum_ref, br, r)
-            return 0
-
-        lax.fori_loop(0, 2, body, 0)
 
     def by_rows(f):
         def body(r, _):
@@ -395,6 +401,9 @@
 
     for j in range(SUB):
         leg1_start(j)
+
+    for i in range(8, 12):
+        loads[i].wait()
 
     def onehot(rows, r):
         ids = lax.broadcasted_iota(jnp.int32, (BLK, E), 0) + r * BLK
@@ -413,28 +422,40 @@
     y_step(0)
     leg1_wait(0)
     leg2_start(0)
-    z_step(2)
-    y_step(1)
     leg2_own(2)
     leg2_own(3)
+    z_step(2)
     leg1_wait(1)
     leg2_start(1)
-    z_step(3)
-    z_step(4)
-    y_step(2)
+    y_step(1)
     leg1_wait(2)
     leg2_start(2)
-    leg2_relay(0)
-    y_step(3)
+    leg2_own(4)
+    leg2_own(5)
     leg1_wait(3)
     leg2_start(3)
+    z_step(3)
+    leg2_own(6)
+    leg2_own(7)
+    z_step(4)
+    leg1_wait(4)
+    leg2_start(4)
+    y_step(2)
+    leg2_relay(0)
+    leg1_wait(5)
+    leg2_start(5)
+    y_step(3)
+    leg1_wait(6)
+    leg2_start(6)
+    leg2_relay(2)
+    leg1_wait(7)
+    leg2_start(7)
     y_step(4)
     finish()
-
     loads[2].wait()
     triplets(g0, aggt.at[0])
     swap_start(0, aggt.at[0], aggm.at[0])
-    leg2_relay(2)
+    leg2_relay(4)
     for i in (3, 4, 5):
         loads[i].wait()
     for r in (0, 1):
@@ -445,14 +466,19 @@
         if r == 0:
             leg2_wait(1)
             leg3_start(1)
+            leg2_wait(3)
+            leg3_start(3)
 
     def part_sum(rows):
         nrm[rows, :] = (summed[rows, :] + branch[rows, :].astype(F32)).astype(BF16)
 
     by_rows(part_sum)
     half1 = proj_t(1, nrm[...])
-    leg2_wait(3)
-    leg3_start(3)
+    leg2_relay(6)
+    leg2_wait(5)
+    leg3_start(5)
+    leg2_wait(7)
+    leg3_start(7)
     swap_wait(1, pbt.at[0], pbm.at[0])
     swap_wait(2, pbt.at[1], pbm.at[1])
     mirrored_pb = jnp.dot(pbm[0], perm[0:256, :], preferred_element_type=F32) + jnp.dot(
@@ -471,7 +497,6 @@
     z_step(3)
     z_step(4)
     y_step(2)
-
     for j in range(SUB):
         leg3_wait(j)
 
@@ -506,14 +531,7 @@
     swap_wait(3, aggt.at[1], aggm.at[1])
     act[0:T, 0:E] = permute_t(aggm[1]).astype(BF16)
     aggm[1] = act[0:T, 0:E]
-    layer(1, mst, aggm.at[1], msum, mbr)
-
-    def final(rows):
-        out_ref[rows, :] = (
-            (summed[rows, :] + branch[rows, :].astype(F32)) + mbr[rows, :].astype(F32)
-        ).astype(BF16)
-
-    by_rows(final)
+    layer(1, mst, aggm.at[1], None, None)
 
     drain0()
     drain1()
@@ -531,12 +549,19 @@
     smem = pl.BlockSpec(memory_space=pltpu.SMEM)
     hbm = pl.BlockSpec(memory_space=pltpu.HBM)
     dma = pltpu.SemaphoreType.DMA
+    def stay(a):
+        return pltpu.with_memory_space_constraint(a, pltpu.HBM)
+
     out = pl.pallas_call(
         kernel,
         out_shape=jax.ShapeDtypeStruct((E, D), BF16),
-        in_specs=[smem, smem, smem, hbm, hbm, vmem, hbm, hbm, hbm, hbm, vmem],
+        in_specs=[hbm, hbm, smem] + [hbm] * 8,
         out_specs=vmem,
         scratch_shapes=[
+            pltpu.SMEM((NB,), jnp.int32),
+            pltpu.SMEM((NB,), jnp.int32),
+            pltpu.VMEM((1, E), jnp.int32),
+            pltpu.VMEM((2, D), F32),
             pltpu.VMEM((E, D), BF16),
             pltpu.VMEM((NB, BLK, BLK), BF16),
             pltpu.VMEM((2, T, D), BF16),
@@ -562,7 +587,7 @@
             pltpu.VMEM((E, D), BF16),
             pltpu.VMEM((E, D), BF16),
             pltpu.VMEM((E, D), BF16),
-            dma((8,)),
+            dma((12,)),
             dma((2,)),
             dma((2, 9, 2)),
             dma((2, 2, 4, 2)),
@@ -574,13 +599,19 @@
             dma((4,)), dma((4,)),
         ],
         compiler_params=pltpu.CompilerParams(
-            collective_id=0, has_side_effects=True, vmem_limit_bytes=56 << 20
+            collective_id=0, has_side_effects=True, vmem_limit_bytes=48 << 20
         ),
         name="edge_layers",
     )(
-        block_target[0, 0], block_source[0, 0], block_count[0], edge_states[0, 0],
-        triplet_coeff[0, 0], reverse_slot[0], jnp.swapaxes(w_proj, 1, 2), w_up, w_in, w_out,
-        norm_gain,
+        *map(stay, (block_target[0, 0], block_source[0, 0])),
+        block_count[0],
+        *map(
+            stay,
+            (
+                reverse_slot[0], norm_gain, edge_states[0, 0], triplet_coeff[0, 0],
+                jnp.swapaxes(w_proj, 1, 2), w_up, w_in, w_out,
+            ),
+        ),
     )
     return out[None, None]
 

time: 91.4 us -> 86.4 us (0.945)
  Pallas kernels: 88.3 us -> 84.7 us
  local copies, waits for them, and re-layouts: 2.26 us -> 0.97 us
    pallas_call x1, Pallas kernels: 88.3 us -> 84.7 us  [local(): pl.pallas_call(kernel, out_shape=jax.ShapeDtypeStruct((E, D), BF16), in_s...]
    unnamed x1, local copies, waits for them, and re-layouts: 2.26 us -> 0.97 us
where the time goes in v5:
time: 86.4 us; the launch traced here: 86.3 us
  Pallas kernels  84.7 us (98%)
  local copies, waits for them, and re-layouts  0.97 us (1%)
    pallas_call x1, Pallas kernels, local(): pl.pallas_call(kernel, out_shape=jax.ShapeDtypeStruct((E, D), BF16), in_s...  84.7 us

profile of v5, /device:TPU:1, one launch (start us, length us, event | category | flops | bytes accessed | tf_op | source)
XLA Modules:
  0.0 86.3 jit_solution(12643772451437603475)
XLA Ops:
  0.7 84.7 %edge_layers.1 = bf16[512,1024]{1,0:T(8,128)(2,1)S(1)} custom-call(s32[16]{0:T(128)} %bitcast.14, s32[16]{0:T(128)} %bitcast.15, s32[1]{0:T(128)} %bitcast.8.cnt_s, s32[1,512]{1,0:T(1,128)} %bitcast.13, f32[2,1024]{1,0:T(2,128)} %gain_h.1, bf16[512,1024]{1,0:T(8,128)(2,1)} %bitcast.10, bf16[16,128,128]{2,1,0:T(8,128)(2,1)} %bitcast.11, ...), custom_call_target="tpu_custom_call" | custom-call | tf_op jit(solution)/shard_map/edge_layers/pallas_call | solution.py:555
  85.4 1.0 %copy.14 = bf16[1,1,512,1024]{3,2,1,0:T(8,128)(2,1)} copy(bf16[1,1,512,1024]{3,2,1,0:T(8,128)(2,1)S(1)} %bitcast.9) | data formatting | bytes 2097152

commit v6 on v5

--- a/solution.py
+++ b/solution.py
@@ -154,11 +154,12 @@
 
         def start():
             for h in (0, 1):
-                own = half(y1, z, h)
                 for direction in (0, 1):
-                    z_copy(own, direction, 1, h).start()
-                y_copy(own, 0, 0, h).start()
-                to_sib(own)
+                    z_copy(half(y1, z, h), direction, 1, h).start()
+            for h in (0, 1):
+                y_copy(half(y1, z, h), 0, 0, h).start()
+            for h in (0, 1):
+                to_sib(half(y1, z, h))
 
         def z_step(dist):
             for h in (0, 1):
@@ -169,8 +170,10 @@
                         z_copy(got, direction, dist + 1, h).start()
                     if dist == 2 and direction == h:
                         z_copy(got, direction, 4, h).start()
-                    y_copy(got, direction, dist, h).start()
-                    to_sib(got)
+                for direction in ways(dist, h):
+                    y_copy(half(y1, origin(direction, dist), h), direction, dist, h).start()
+                for direction in ways(dist, h):
+                    to_sib(half(y1, origin(direction, dist), h))
 
         def y_step(dist):
             for h in (0, 1):

time: 86.4 us -> 86.3 us (level)
  no operation moved by 1% of the time
where the time goes in v6:
time: 86.3 us; the launch traced here: 86.2 us
  Pallas kernels  84.6 us (98%)
  local copies, waits for them, and re-layouts  0.97 us (1%)
    pallas_call x1, Pallas kernels, local(): pl.pallas_call(kernel, out_shape=jax.ShapeDtypeStruct((E, D), BF16), in_s...  84.6 us

profile of v6, /device:TPU:1, one launch (start us, length us, event | category | flops | bytes accessed | tf_op | source)
XLA Modules:
  0.0 86.2 jit_solution(6715796220113602167)
XLA Ops:
  0.7 84.6 %edge_layers.1 = bf16[512,1024]{1,0:T(8,128)(2,1)S(1)} custom-call(s32[16]{0:T(128)} %bitcast.14, s32[16]{0:T(128)} %bitcast.15, s32[1]{0:T(128)} %bitcast.8.cnt_s, s32[1,512]{1,0:T(1,128)} %bitcast.13, f32[2,1024]{1,0:T(2,128)} %gain_h.1, bf16[512,1024]{1,0:T(8,128)(2,1)} %bitcast.10, bf16[16,128,128]{2,1,0:T(8,128)(2,1)} %bitcast.11, ...), custom_call_target="tpu_custom_call" | custom-call | tf_op jit(solution)/shard_map/edge_layers/pallas_call | solution.py:558
  85.3 1.0 %copy.14 = bf16[1,1,512,1024]{3,2,1,0:T(8,128)(2,1)} copy(bf16[1,1,512,1024]{3,2,1,0:T(8,128)(2,1)S(1)} %bitcast.9) | data formatting | bytes 2097152
